TPU v7x, 512 devices: a whole 4x4x16 slice. The times are simulated.
512 devices in a mesh: row: 128 (over x, z_hi, y, core), col: 4 (over z_lo).
Axes of the slice: x: 4, y: 4, z: 16 (z_hi: 4, z_lo: 4; z = z_hi * 4 + z_lo), core: 2. Of those that a mesh axis runs over, the one named last changes fastest.
Arguments:
- state: bfloat16 [4, 512, 512, 128], P('col', 'row'), may hold values from -6 to 6
- accum: float32 [4, 512, 512, 128], P('col', 'row'), may hold values from -6 to 6
- poisson_weight: float32 [1], replicated, may hold values from 0.2 to 1
- route1_blocks: bfloat16 [2, 8, 4, 64, 64], replicated, may hold values from -0.25 to 0.25
- route1_cols: int32 [2, 8, 4], replicated, may hold values from 0 to 7, as said below
- route2_blocks: bfloat16 [5, 8, 4, 64, 64], replicated, may hold values from -0.25 to 0.25
- route2_cols: int32 [5, 8, 4], replicated, may hold values from 0 to 7, as said below
- route3_factors: bfloat16 [2, 128, 128], replicated, may hold values from -0.375 to 0.375
- fleet_offsets: int32 [3], replicated, may hold values from -1 to 1, as said below
Outputs:
- next_state: bfloat16 [4, 512, 512, 128], P('col', 'row')
- next_accum: float32 [4, 512, 512, 128], P('col', 'row')
Inputs may be any that keep to these rules, and one draw needn't show every extreme that they name: `route1_cols`: within each block row of each factor the 4 block columns are distinct. `route2_cols`: within each block row of each factor the 4 block columns are distinct. `fleet_offsets`: both -1 and +1 occur among the offsets.
All inputs are finite; a program needn't handle non-finite values.
Results may differ from a plain program's by a relative error of at most 0.0025.
Values may be sent and summed in bfloat16 or wider, within the bound.
No kernel may reach another device: no remote copies, remote signals or barrier semaphores. Data moves between devices by JAX's collectives and lax.ppermute only.
A program may use at most 64 MiB of HBM per device.

v0:
```python
import jax
import jax.numpy as jnp
from jax import lax
from jax.sharding import PartitionSpec as P


def padded_2(value, sides, width):
    for axis, dim in sides:
        devices, length = (lax.axis_size(axis), value.shape[dim])
        up = [(i, (i + 1) % devices) for i in range(devices - 1)]
        down = [(j, i) for i, j in up]
        last = lax.slice_in_dim(value, length - width, length, axis=dim)
        first = lax.slice_in_dim(value, 0, width, axis=dim)
        before = lax.ppermute(last, axis, up)
        after = lax.ppermute(first, axis, down)
        value = jnp.concatenate([before, value, after], axis=dim)
    return value


def densify(blocks, columns):
    count = blocks.shape[0]
    width = blocks.shape[2]
    onehot = (columns[:, :, None] == jnp.arange(count, dtype=jnp.int32)[None, None, :]).astype(
        jnp.float32
    )
    dense = jnp.einsum("rkij,rkc->ricj", blocks.astype(jnp.float32), onehot)
    return dense.reshape(count * width, count * width).astype(jnp.bfloat16)


def along_first(matrix, field):
    return jnp.einsum("ab,fbmc->famc", matrix, field, preferred_element_type=jnp.float32)


def along_second(matrix, field):
    return jnp.einsum("mn,fanc->famc", matrix, field, preferred_element_type=jnp.float32)


def along_third(matrix, field):
    return jnp.einsum("cd,famd->famc", matrix, field, preferred_element_type=jnp.float32)


def local(
    state,
    accum,
    poisson_weight,
    route1_blocks,
    route1_cols,
    route2_blocks,
    route2_cols,
    route3_factors,
    fleet_offsets,
):
    first_local = densify(route1_blocks[0], route1_cols[0])
    first_sync = densify(route1_blocks[1], route1_cols[1])
    second_all = [
        densify(route2_blocks[term], route2_cols[term]) for term in range(route2_blocks.shape[0])
    ]
    levels_here = state.shape[0]
    sectioned = along_third(route3_factors[1], state).astype(jnp.bfloat16)
    coupled = along_second(second_all[1], sectioned).astype(jnp.bfloat16)
    exchanged = (
        lax.all_to_all(state, "row", split_axis=2, concat_axis=1, tiled=True),
        lax.all_to_all(coupled, "row", split_axis=2, concat_axis=1, tiled=True),
    )
    first_terms = along_first(first_local, exchanged[0]) + along_first(first_sync, exchanged[1])
    returned = lax.all_to_all(first_terms, "row", split_axis=1, concat_axis=2, tiled=True)
    total = state.astype(jnp.float32) + returned + along_second(second_all[0], state)
    total = total + along_third(route3_factors[0], state)
    padded = padded_2(state, (("col", 0),), 1)
    base_level = jnp.zeros((), jnp.int32)
    for term_index in range(len(second_all) - 2):
        start = base_level + 1 - fleet_offsets[term_index]
        source = lax.dynamic_slice_in_dim(padded, start, levels_here, 0)
        total = total + along_second(second_all[2 + term_index], source)
    return (total.astype(jnp.bfloat16), accum + poisson_weight[0] * total)


def solution(mesh):
    placed = (
        P("col", "row", None, None),
        P("col", "row", None, None),
        P(),
        P(),
        P(),
        P(),
        P(),
        P(),
        P(),
    )
    return jax.shard_map(
        local,
        mesh=mesh,
        in_specs=placed,
        out_specs=(P("col", "row", None, None), P("col", "row", None, None)),
        check_vma=False,
    )
```

profile of v0, /device:TPU:1, one launch (start us, length us, event | category | flops | bytes accessed | tf_op | source)
XLA Modules:
  0.0 181.2 jit_solution(5288352626844702676)
XLA Ops:
  0.6 2.3 %copy.63 = bf16[1,4,512,128]{3,1,0,2:T(4,128)(2,1)} copy(bf16[1,4,512,128]{3,2,1,0:T(8,128)(2,1)} %param.9) | data formatting | bytes 1048576 | tf_op args[0]
  2.9 23.5 %all-to-all-start = ((bf16[1,4,512,128]{3,1,0,2:T(4,128)(2,1)}), bf16[1,4,512,128]{3,1,0,2:T(4,128)(2,1)}, u32[]{:S(2)}, u32[]{:S(2)}) async-start(bf16[1,4,512,128]{3,1,0,2:T(4,128)(2,1)} %copy.63), calls=%async_computation | async-start | bytes 1048576 | tf_op jit(solution)/shard_map/all_to_all | solution.py:62
  26.4 0.1 copy.65
  26.5 3.4 %fusion.54 = (bf16[1,8,4,64,64]{4,3,2,1,0:T(8,128)(2,1)S(1)}, bf16[1,8,4,64,64]{4,3,2,1,0:T(8,128)(2,1)}, bf16[1,8,4,64,64]{4,3,2,1,0:T(8,128)(2,1)}, bf16[1,8,4...) fusion(bf16[5,8,4,64,64]{4,3,2,1,0:T(8,128)(2,1)} %param.14), kind=kLoop, calls=%fused_computation.85 | loop fusion | bytes 2621440 | tf_op jit(solution)/shard_map/slice | solution.py:56
  29.9 0.7 fusion.1
  30.6 0.6 reshape.85
  31.2 0.0 copy-done
  31.2 0.0 copy-done.12
  31.2 0.0 copy-start.15
  31.2 0.7 fusion.13
  31.9 1.1 copy.68
  33.0 24.2 %all-to-all-done = bf16[1,4,512,128]{3,1,0,2:T(4,128)(2,1)} async-done(((bf16[1,4,512,128]{3,1,0,2:T(4,128)(2,1)}), bf16[1,4,512,128]{3,1,0,2:T(4,128)(2,1)}, u32[]{:S(2)}, u32[]{:S(2)}) %all-to-all-start) | async-done | bytes 524320 | tf_op jit(solution)/shard_map/all_to_all | solution.py:62
  57.2 11.8 %all-to-all-start.1 = ((bf16[1,4,512,128]{3,1,0,2:T(4,128)(2,1)}), bf16[1,4,512,128]{3,1,0,2:T(4,128)(2,1)S(1)}, u32[]{:S(2)}, u32[]{:S(2)}) async-start(bf16[1,4,512,128]{3,1,0,2:T(4,128)(2,1)} %copy.68), calls=%async_computation.1 | async-start | bytes 1048576 | tf_op jit(solution)/shard_map/all_to_all | solution.py:63
  69.1 0.0 copy-done.15
  69.1 0.1 copy.71
  69.2 0.1 copy.61
  69.2 0.9 fusion.55
  70.1 0.6 fusion.2
  70.8 1.4 reshape.87
  72.2 1.7 fusion
  73.9 1.4 reshape.82
  75.3 2.1 %copy.64 = bf16[1,4,128,4,128]{4,1,2,3,0:T(4,128)(2,1)} copy(bf16[1,4,128,4,128]{4,1,3,2,0:T(4,128)(2,1)} %bitcast.5) | data formatting | bytes 1048576 | tf_op jit(solution)/shard_map/all_to_all | solution.py:62
  77.4 22.9 %all-to-all-done.1 = bf16[1,4,512,128]{3,1,0,2:T(4,128)(2,1)S(1)} async-done(((bf16[1,4,512,128]{3,1,0,2:T(4,128)(2,1)}), bf16[1,4,512,128]{3,1,0,2:T(4,128)(2,1)S(1)}, u32[]{:S(2)}, u32[]{:S(2)}) %all-to-all-start.1) | async-done | bytes 524320 | tf_op jit(solution)/shard_map/all_to_all | solution.py:63
  100.4 0.1 copy.69
  100.5 0.4 copy.70
  100.9 0.5 copy-done.9
  101.4 0.4 convolution_bitcast_fusion.5
  101.9 0.4 fusion.7
  102.3 1.7 copy.75
  104.0 12.3 %all-to-all-start.2 = ((f32[1,512,4,128]{3,2,0,1:T(4,128)}), f32[1,512,4,128]{3,2,0,1:T(4,128)}, u32[]{:S(2)}, u32[]{:S(2)}) async-start(f32[1,512,4,128]{3,2,0,1:T(4,128)} %copy.75), calls=%async_computation.2 | async-start | bytes 2097152 | tf_op jit(solution)/shard_map/all_to_all | solution.py:66
  116.3 4.2 %collective-permute-start = (bf16[1,4,512,128]{3,2,1,0:T(8,128)(2,1)S(1)}, bf16[1,4,512,128]{3,2,1,0:T(8,128)(2,1)}, u32[]{:S(2)}, u32[]{:S(2)}) collective-permute-start(bf16[1,4,512,128]{3,2,1,0:T(8,128)(2,1)S(1)} %copy-done), channel_id=1, source_target_pairs={{0,1},{1,2},{2,3},{4,5},{5,6},{6,7},{8,9},{9,10},{10,11},{12,13},{... | collective-permute-start | bytes 1572872 | tf_op jit(solution)/shard_map/ppermute | solution.py:14
  120.5 1.3 collective-permute-start.1
  121.8 0.1 copy.80
  121.9 0.1 copy.77
  122.0 0.1 copy.84
  122.1 0.6 fusion.4
  122.7 0.0 copy-start.14
  122.7 1.7 fusion.5
  124.4 1.6 fusion.3
  126.1 0.6 fusion.56
  131.1 0.1 copy.88
  131.2 1.4 reshape.92
  132.6 1.4 reshape.94
  134.0 1.4 reshape.89
  135.4 0.6 fusion.6
  136.1 0.6 reshape.96
  136.7 0.0 copy-start.5
  136.7 34.3 %collective-permute-done = bf16[1,4,512,128]{3,2,1,0:T(8,128)(2,1)} collective-permute-done((bf16[1,4,512,128]{3,2,1,0:T(8,128)(2,1)S(1)}, bf16[1,4,512,128]{3,2,1,0:T(8,128)(2,1)}, u32[]{:S(2)}, u32[]{:S(2)}) %collective-permute-start) | collective-permute-done | bytes 524320 | tf_op jit(solution)/shard_map/ppermute | solution.py:14
  171.0 1.1 constant_dynamic-update-slice_fusion.2
  172.1 0.1 constant_dynamic-update-slice_fusion.1
  172.2 0.1 collective-permute-done.1
  172.3 1.1 constant_dynamic-update-slice_fusion
  173.4 0.4 convolution_bitcast_fusion.2
  173.9 0.7 copy-done.2
  174.6 0.4 convolution_bitcast_fusion.1
  175.0 0.0 copy-start.6
  175.1 0.0 all-to-all-done.2
  175.1 1.5 copy.76
  176.5 0.4 fusion.9
  177.0 0.0 copy-start.11
  177.0 0.3 fusion.8
  177.3 0.7 copy-done.4
  178.0 0.3 copy-done.11
  178.4 2.8 %multiply_add_fusion = (f32[1,4,512,128]{3,2,1,0:T(8,128)}, bf16[1,4,512,128]{3,2,1,0:T(8,128)(2,1)}) fusion(f32[1,4,512,128]{3,2,1,0:T(8,128)S(1)} %copy-done.11, f32[]{:T(128)} %bitcast.197, f32[1,4,512,128]{3,2,1,0:T(8,128)S(1)} %convolution_bitcast_fusion.1, f32[1,4,512,128]{3,2,1,0:T(8,128)S(1)} %convolution_bitcast_fusion.2, ...), kind=kOutput, calls=%fused_computation.30 | convolution fusion | flops 270008320 | bytes 6816260 | tf_op jit(solution)/shard_map/mn,fanc->famc/dot_general | solution.py:35
  (22 shorter events, 0.0 us)
Async XLA Ops:
  0.6 25.8 %copy-start.13 = (s32[5,8,4]{1,2,0:T(4,128)S(1)}, s32[5,8,4]{1,2,0:T(4,128)}, u32[]{:S(2)}) copy-start(s32[5,8,4]{1,2,0:T(4,128)} %param.15) | copy-start | bytes 1924
  2.9 54.3 %all-to-all-start = ((bf16[1,4,512,128]{3,1,0,2:T(4,128)(2,1)}), bf16[1,4,512,128]{3,1,0,2:T(4,128)(2,1)}, u32[]{:S(2)}, u32[]{:S(2)}) async-start(bf16[1,4,512,128]{3,1,0,2:T(4,128)(2,1)} %copy.63), calls=%async_computation | async-start | bytes 1048576 | tf_op jit(solution)/shard_map/all_to_all | solution.py:62
  29.9 1.3 copy-start
  29.9 1.3 copy-start.12
  31.2 37.9 %copy-start.15 = (s32[2,8,4]{1,2,0:T(4,128)S(1)}, s32[2,8,4]{1,2,0:T(4,128)}, u32[]{:S(2)}) copy-start(s32[2,8,4]{1,2,0:T(4,128)} %param.13) | copy-start | bytes 772
  33.0 36.2 %copy-start.10 = (bf16[2,8,4,64,64]{4,3,2,1,0:T(8,128)(2,1)S(1)}, bf16[2,8,4,64,64]{4,3,2,1,0:T(8,128)(2,1)}, u32[]{:S(2)}) copy-start(bf16[2,8,4,64,64]{4,3,2,1,0:T(8,128)(2,1)} %param.12) | copy-start | bytes 1572868
  57.2 43.1 %all-to-all-start.1 = ((bf16[1,4,512,128]{3,1,0,2:T(4,128)(2,1)}), bf16[1,4,512,128]{3,1,0,2:T(4,128)(2,1)S(1)}, u32[]{:S(2)}, u32[]{:S(2)}) async-start(bf16[1,4,512,128]{3,1,0,2:T(4,128)(2,1)} %copy.68), calls=%async_computation.1 | async-start | bytes 1048576 | tf_op jit(solution)/shard_map/all_to_all | solution.py:63
  75.3 25.5 %copy-start.8 = (bf16[512,512,1]{1,0,2:T(8,128)(2,1)S(1)}, bf16[512,512,1]{1,0,2:T(8,128)(2,1)}, u32[]{:S(2)}) copy-start(bf16[512,512,1]{1,0,2:T(8,128)(2,1)} %reshape.82) | copy-start | bytes 1572868
  100.4 1.0 copy-start.9
  100.4 1.4 copy-start.7
  104.0 71.1 %all-to-all-start.2 = ((f32[1,512,4,128]{3,2,0,1:T(4,128)}), f32[1,512,4,128]{3,2,0,1:T(4,128)}, u32[]{:S(2)}, u32[]{:S(2)}) async-start(f32[1,512,4,128]{3,2,0,1:T(4,128)} %copy.75), calls=%async_computation.2 | async-start | bytes 2097152 | tf_op jit(solution)/shard_map/all_to_all | solution.py:66
  116.3 54.7 %collective-permute-start = (bf16[1,4,512,128]{3,2,1,0:T(8,128)(2,1)S(1)}, bf16[1,4,512,128]{3,2,1,0:T(8,128)(2,1)}, u32[]{:S(2)}, u32[]{:S(2)}) collective-permute-start(bf16[1,4,512,128]{3,2,1,0:T(8,128)(2,1)S(1)} %copy-done), channel_id=1, source_target_pairs={{0,1},{1,2},{2,3},{4,5},{5,6},{6,7},{8,9},{9,10},{10,11},{12,13},{... | collective-permute-start | bytes 1572872 | tf_op jit(solution)/shard_map/ppermute | solution.py:14
  120.5 51.8 %collective-permute-start.1 = (bf16[1,4,512,128]{3,2,1,0:T(8,128)(2,1)S(1)}, bf16[1,4,512,128]{3,2,1,0:T(8,128)(2,1)}, u32[]{:S(2)}, u32[]{:S(2)}) collective-permute-start(bf16[1,4,512,128]{3,2,1,0:T(8,128)(2,1)S(1)} %copy-done), channel_id=1, source_target_pairs={{1,0},{2,1},{3,2},{5,4},{6,5},{7,6},{9,8},{10,9},{11,10},{13,12},{... | collective-permute-start | bytes 1572872 | tf_op jit(solution)/shard_map/ppermute | solution.py:15
  122.1 2.4 %copy-start.3 = (bf16[1,8,4,64,64]{4,3,2,1,0:T(8,128)(2,1)S(1)}, bf16[1,8,4,64,64]{4,3,2,1,0:T(8,128)(2,1)}, u32[]{:S(2)}) copy-start(bf16[1,8,4,64,64]{4,3,2,1,0:T(8,128)(2,1)} %get-tuple-element.4) | copy-start | bytes 786436
  122.7 3.4 %copy-start.14 = (s32[3]{0:T(128)S(1)}, s32[3]{0:T(128)}, u32[]{:S(2)}) copy-start(s32[3]{0:T(128)} %param.17) | copy-start | bytes 40
  132.6 1.4 copy-start.1
  136.7 36.7 %copy-start.5 = (bf16[512,512,1]{1,0,2:T(8,128)(2,1)S(1)}, bf16[512,512,1]{1,0,2:T(8,128)(2,1)}, u32[]{:S(2)}) copy-start(bf16[512,512,1]{1,0,2:T(8,128)(2,1)} %reshape.94) | copy-start | bytes 1572868
  173.4 1.2 copy-start.2
  175.0 1.5 copy-start.6
  177.0 1.0 copy-start.4
  177.0 1.4 copy-start.11
where the time goes:
time: 183 us; the launch traced here: 181 us
  waiting for transfers between devices  81.6 us (45%)
  starting transfers between devices  53.1 us (29%)
  local copies, waits for them, and re-layouts  27.4 us (15%)
  matrix products  13.6 us (7%)
  between operations  5.44 us (3%)
    ppermute x1, waiting for transfers between devices, padded_2(): before = lax.ppermute(last, axis, up)  34.3 us
    all_to_all x1, waiting for transfers between devices, local(): lax.all_to_all(state, 'row', split_axis=2, concat_axis=1, tiled=True)  24.2 us
    all_to_all x1, starting transfers between devices, local(): lax.all_to_all(state, 'row', split_axis=2, concat_axis=1, tiled=True)  23.5 us
    all_to_all x1, waiting for transfers between devices, local(): lax.all_to_all(coupled, 'row', split_axis=2, concat_axis=1, tiled=True)  22.9 us
    all_to_all x1, starting transfers between devices, local(): lax.all_to_all(first_terms, 'row', split_axis=1, concat_axis=2, tiled=True)  12.3 us
    all_to_all x1, starting transfers between devices, local(): lax.all_to_all(coupled, 'row', split_axis=2, concat_axis=1, tiled=True)  11.8 us
    convert_element_type x7, local copies, waits for them, and re-layouts, densify(): return dense.reshape(count * width, count * width).astype(jnp.bfloat16)  8.26 us
    dot_general x7, matrix products, densify(): dense = jnp.einsum('rkij,rkc->ricj', blocks.astype(jnp.float32), onehot)  7.63 us
  transfers between devices with their start and end apart: 5, of which 4 were waited for; matrix products, arithmetic and copies ran while one was open for 16% of the time, Pallas kernels for 0%

commit v1 on v0

v1 whole, which is shorter than its diff:
```python
import jax
import jax.numpy as jnp
from jax import lax
from jax.experimental import pallas as pl
from jax.experimental.pallas import tpu as pltpu
from jax.sharding import PartitionSpec as P

NX, NZ, NY, NC = 4, 4, 4, 2
PLANE = NX * NY * NC
BF = jnp.bfloat16
F32 = jnp.float32


def row_of(x, z, y, core):
    return ((x * NZ + z % NZ) * NY + y) * NC + core


def plane_groups():
    return [
        [row_of(x, z, y, c) for x in range(NX) for y in range(NY) for c in range(NC)]
        for z in range(NZ)
    ]


def z_shift(step):
    return [
        (row_of(x, z, y, c), row_of(x, z + step, y, c))
        for x in range(NX)
        for z in range(NZ)
        for y in range(NY)
        for c in range(NC)
    ]


def cost(flops, moved):
    return pl.CostEstimate(flops=flops, bytes_accessed=moved, transcendentals=0)


SMALL = pltpu.CompilerParams(vmem_limit_bytes=24 * 1024 * 1024)


def iota2(shape):
    return (
        lax.broadcasted_iota(jnp.int32, shape, 0),
        lax.broadcasted_iota(jnp.int32, shape, 1),
    )


def onehot(rows_match):
    return jnp.where(rows_match, 1.0, 0.0).astype(BF)


def dot(a, b):
    return jnp.dot(a, b, preferred_element_type=F32)


def factors_kernel(cols1, cols2, own, b1, b2, second, sync2, first, dense):
    second[...] = jnp.zeros_like(second)
    sync2[...] = jnp.zeros_like(sync2)
    dense[...] = jnp.zeros_like(dense)

    def place(dst, r, base, c, blk):
        zero = jnp.zeros_like(blk)
        left = jnp.concatenate([blk, zero], axis=1)
        right = jnp.concatenate([zero, blk], axis=1)
        wide = jnp.where((c & 1) == 0, left, right)
        at = (
            pl.ds(pl.multiple_of(r * 64, 64), 64),
            pl.ds(pl.multiple_of(base + (c >> 1) * 128, 128), 128),
        )
        dst[at] = dst[at] + wide

    def row(r, carry):
        for k in range(4):
            for t in range(2):
                place(dense.at[t], r, 0, cols1[t * 32 + r * 4 + k], b1[t, r, k])
            place(sync2, r, 0, cols2[32 + r * 4 + k], b2[1, r, k])
            for t, base in ((0, 0), (2, 512), (3, 1024), (4, 1536)):
                place(second, r, base, cols2[t * 32 + r * 4 + k], b2[t, r, k])
        return carry

    lax.fori_loop(0, 8, row, 0)
    me = own[0]
    i, j = iota2((512, 512))
    source = ((j >> 5) & 3) * 128 + (j >> 7) * 32 + (j & 31)
    swap = onehot(i == source)
    for t in range(2):
        rows = jnp.concatenate(
            [dense[t, pl.ds(pl.multiple_of(x * 128 + me * 32, 32), 32), :] for x in range(4)],
            axis=0,
        )
        turned = dot(rows, swap).astype(BF)
        for z in range(4):
            slot = (z - me + 4) & 3
            first[t, slot] = turned[:, z * 128 : (z + 1) * 128]


def factors(cols1, cols2, own, b1, b2):
    smem = pl.BlockSpec(memory_space=pltpu.SMEM)
    vmem = pl.BlockSpec(memory_space=pltpu.VMEM)
    return pl.pallas_call(
        factors_kernel,
        out_shape=(
            jax.ShapeDtypeStruct((512, 2048), BF),
            jax.ShapeDtypeStruct((512, 512), BF),
            jax.ShapeDtypeStruct((2, 4, 128, 128), BF),
        ),
        in_specs=[smem, smem, smem, vmem, vmem],
        out_specs=(vmem, vmem, vmem),
        scratch_shapes=[pltpu.VMEM((2, 512, 512), BF)],
        cost_estimate=cost(300_000_000, 8_000_000),
        compiler_params=SMALL,
        name="factors",
    )(cols1, cols2, own, b1, b2)


def arrange_kernel(got, half_a, half_b):
    i, j = iota2((256, 256))
    move = onehot(j == ((i >> 2) & 3) * 64 + (i & 3) * 16 + (i >> 4))
    for g in range(8):
        block = got[4 * g : 4 * g + 4].reshape(256, 128)
        out = dot(move, block).astype(BF)
        for m in range(16):
            dst = half_a if m < 8 else half_b
            dst[m % 8, g * 16 : g * 16 + 16, :] = out[m * 16 : m * 16 + 16, :]


def arrange(got):
    half = jax.ShapeDtypeStruct((8, 128, 128), BF)
    return pl.pallas_call(
        arrange_kernel,
        out_shape=(half, half),
        cost_estimate=cost(130_000_000, 1_100_000),
        compiler_params=SMALL,
        name="arrange",
    )(got)


def pair_products(first, s3_twice, slot, half, p, add1, add2):
    x = jnp.concatenate([half[2 * p], half[2 * p + 1]], axis=1)
    section = dot(x, s3_twice).astype(BF)
    one = dot(first[0, slot], x)
    two = dot(first[1, slot], section)
    if add1 is not None:
        one, two = one + add1, two + add2
    return one, two


def twice(s3):
    zero = jnp.zeros_like(s3)
    return jnp.concatenate(
        [jnp.concatenate([s3, zero], axis=1), jnp.concatenate([zero, s3], axis=1)], axis=0
    )


def near_kernel(first, s3, a0, b0, a3, b3, a1, b1, acc):
    s3_twice = twice(s3[...])
    for h, halves in enumerate(((a0, a3, a1), (b0, b3, b1))):
        for p in range(4):
            one, two = None, None
            for slot, half in zip((0, 3, 1), halves):
                one, two = pair_products(first, s3_twice, slot, half, p, one, two)
            at = (h * 4 + p) * 256
            acc[0, :, at : at + 256] = one
            acc[1, :, at : at + 256] = two


def near(first, s3, pieces):
    return pl.pallas_call(
        near_kernel,
        out_shape=jax.ShapeDtypeStruct((2, 128, 2048), F32),
        cost_estimate=cost(800_000_000, 4_000_000),
        compiler_params=SMALL,
        name="near",
    )(first, s3, *pieces)


def far_kernel(first, s3, acc, a2, b2, out, keep):
    s3_twice = twice(s3[...])
    for h, half in enumerate((a2, b2)):
        for p in range(4):
            at = (h * 4 + p) * 256
            one, two = pair_products(
                first, s3_twice, 2, half, p, acc[0, :, at : at + 256], acc[1, :, at : at + 256]
            )
            keep[0, :, at : at + 256] = one.astype(BF)
            keep[1, :, at : at + 256] = two.astype(BF)
    i, j = iota2((256, 256))
    move = onehot(i == ((j >> 2) & 3) * 64 + (j & 3) * 16 + (j >> 4))
    for t in range(2):
        for g in range(8):
            rows = jnp.concatenate(
                [keep[t, g * 16 : g * 16 + 16, m * 128 : m * 128 + 128] for m in range(16)],
                axis=0,
            )
            out[4 * g : 4 * g + 4, t] = dot(move, rows).astype(BF).reshape(4, 64, 128)


def far(first, s3, acc, a2, b2):
    return pl.pallas_call(
        far_kernel,
        out_shape=jax.ShapeDtypeStruct((32, 2, 64, 128), BF),
        scratch_shapes=[pltpu.VMEM((2, 128, 2048), BF)],
        cost_estimate=cost(400_000_000, 4_000_000),
        compiler_params=SMALL,
        name="far",
    )(first, s3, acc, a2, b2)


def local_kernel(offsets, second, r3, state, before, after, out, stack):
    x = state[0]
    stack[0:512, :] = x
    for k in range(3):
        off = offsets[k]
        rows = slice(512 * (k + 1), 512 * (k + 2))

        @pl.when(off == 1)
        def _():
            stack[rows, :] = before[0]

        @pl.when(off == 0)
        def _():
            stack[rows, :] = state[0]

        @pl.when(off == -1)
        def _():
            stack[rows, :] = after[0]

    out[0] = x.astype(F32) + dot(x, r3[...]) + dot(second[...], stack[...])


def local_terms(offsets, second, r3, state, before, after):
    slab = pl.BlockSpec((1, 512, 128), lambda b: (b, 0, 0))
    return pl.pallas_call(
        local_kernel,
        grid=(4,),
        out_shape=jax.ShapeDtypeStruct((4, 512, 128), F32),
        in_specs=[
            pl.BlockSpec(memory_space=pltpu.SMEM),
            pl.BlockSpec((512, 2048), lambda b: (0, 0)),
            pl.BlockSpec((128, 128), lambda b: (0, 0)),
            slab,
            slab,
            slab,
        ],
        out_specs=slab,
        scratch_shapes=[pltpu.VMEM((2048, 128), BF)],
        cost_estimate=cost(1_200_000_000, 5_000_000),
        compiler_params=SMALL,
        name="local_terms",
    )(offsets, second, r3, state, before, after)


def finish_kernel(weight, sync2, back, base, accum, state_out, accum_out):
    one = back[:, 0, 0].reshape(512, 128)
    two = back[:, 1, 0].reshape(512, 128)
    total = base[0] + one.astype(F32) + dot(sync2[...], two)
    state_out[0] = total.astype(BF)
    accum_out[0] = accum[0] + weight[0] * total


def finish(weight, sync2, back, base, accum):
    slab = pl.BlockSpec((1, 512, 128), lambda b: (b, 0, 0))
    return pl.pallas_call(
        finish_kernel,
        grid=(4,),
        out_shape=(
            jax.ShapeDtypeStruct((4, 512, 128), BF),
            jax.ShapeDtypeStruct((4, 512, 128), F32),
        ),
        in_specs=[
            pl.BlockSpec(memory_space=pltpu.SMEM),
            pl.BlockSpec((512, 512), lambda b: (0, 0)),
            pl.BlockSpec((32, 2, 1, 16, 128), lambda b: (0, 0, b, 0, 0)),
            slab,
            slab,
        ],
        out_specs=(slab, slab),
        cost_estimate=cost(300_000_000, 6_000_000),
        compiler_params=SMALL,
        name="finish",
    )(weight, sync2, back, base, accum)


def local(
    state,
    accum,
    poisson_weight,
    route1_blocks,
    route1_cols,
    route2_blocks,
    route2_cols,
    route3_factors,
    fleet_offsets,
):
    field = state[0]
    levels = lax.axis_size("col")
    up = [(i, i + 1) for i in range(levels - 1)]
    down = [(i + 1, i) for i in range(levels - 1)]
    before = lax.ppermute(field, "col", up)
    after = lax.ppermute(field, "col", down)
    groups = plane_groups()

    split = field.reshape(4, PLANE, 16, 128).transpose(1, 0, 2, 3).reshape(PLANE, 64, 128)
    got = lax.all_to_all(split, "row", 0, 0, tiled=True, axis_index_groups=groups)
    got, before, after = lax.optimization_barrier((got, before, after))
    a0, b0 = arrange(got)

    plus, minus = z_shift(1), z_shift(-1)
    a3 = lax.ppermute(a0, "row", plus)
    b1 = lax.ppermute(b0, "row", minus)
    b3 = lax.ppermute(b0, "row", plus)
    a1 = lax.ppermute(a0, "row", minus)
    a2 = lax.ppermute(a3, "row", plus)
    b2 = lax.ppermute(b1, "row", minus)

    own = (lax.axis_index("row") // (NY * NC)) % NZ
    second, sync2, first = factors(
        route1_cols.reshape(-1),
        route2_cols.reshape(-1),
        own.astype(jnp.int32).reshape(1),
        route1_blocks,
        route2_blocks,
    )
    turned = jnp.swapaxes(route3_factors, 1, 2)
    base = local_terms(fleet_offsets, second, turned[0], field, before, after)
    acc = near(first, turned[1], (a0, b0, a3, b3, a1, b1))
    sent = far(first, turned[1], acc, a2, b2)
    back = lax.all_to_all(
        sent.reshape(PLANE, 128, 128), "row", 0, 0, tiled=True, axis_index_groups=groups
    ).reshape(PLANE, 2, 4, 16, 128)
    state_out, accum_out = finish(poisson_weight, sync2, back, base, accum[0])
    return state_out[None], accum_out[None]


def solution(mesh):
    placed = (
        P("col", "row", None, None),
        P("col", "row", None, None),
        P(),
        P(),
        P(),
        P(),
        P(),
        P(),
        P(),
    )
    return jax.shard_map(
        local,
        mesh=mesh,
        in_specs=placed,
        out_specs=(P("col", "row", None, None), P("col", "row", None, None)),
        check_vma=False,
    )
```

time: 183 us -> 147 us (0.80)
  the two profiles are of different devices: /device:TPU:1 before, /device:TPU:65 now
where the time goes in v1:
time: 147 us; the launch traced here: 146 us
  waiting for transfers between devices  56 us (38%)
  starting transfers between devices  40.6 us (28%)
  blocking collectives  19.7 us (13%)
  Pallas kernels  16.8 us (11%)
  local copies, waits for them, and re-layouts  11.5 us (8%)
  between operations  1.57 us (1%)
    ppermute x1, waiting for transfers between devices, local(): a3 = lax.ppermute(a0, 'row', plus)  23.5 us
    ppermute x1, waiting for transfers between devices, local(): b2 = lax.ppermute(b1, 'row', minus)  19.8 us
    all_to_all x1, blocking collectives, local(): lax.all_to_all(split, 'row', 0, 0, tiled=True, axis_index_groups=groups)  19.7 us
    unnamed x29, local copies, waits for them, and re-layouts  10.2 us
    all_to_all x1, waiting for transfers between devices, local(): lax.all_to_all(sent.reshape(PLANE, 128, 128), 'row', 0, 0, tiled=True, ax...  9.79 us
    ppermute x1, starting transfers between devices, local(): a3 = lax.ppermute(a0, 'row', plus)  8.8 us
    ppermute x1, starting transfers between devices, local(): a1 = lax.ppermute(a0, 'row', minus)  7.28 us
    ppermute x1, starting transfers between devices, local(): b2 = lax.ppermute(b1, 'row', minus)  4.78 us
  transfers between devices with their start and end apart: 9, of which 5 were waited for; matrix products, arithmetic and copies ran while one was open for 2% of the time, Pallas kernels for 7%

profile of v1, /device:TPU:65, one launch (start us, length us, event | category | flops | bytes accessed | tf_op | source)
XLA Modules:
  0.0 146.2 jit_solution(14088430424810391590)
XLA Ops:
  0.6 0.0 copy-start.12
  0.6 0.0 copy-start.11
  0.7 0.0 copy-start
  0.7 2.2 %collective-permute-start.1 = (bf16[4,512,128]{2,1,0:T(8,128)(2,1)}, bf16[4,512,128]{2,1,0:T(8,128)(2,1)S(1)}, u32[]{:S(2)}, u32[]{:S(2)}) collective-permute-start(bf16[4,512,128]{2,1,0:T(8,128)(2,1)} %bitcast.17), channel_id=1, source_target_pairs={{1,0},{2,1},{3,2},{5,4},{6,5},{7,6},{9,8},{10,9},{11,10},{13,12},{... | collective-permute-start | bytes 1572872 | tf_op jit(solution)/shard_map/ppermute | solution.py:301
  2.9 3.4 %collective-permute-start = (bf16[4,512,128]{2,1,0:T(8,128)(2,1)}, bf16[4,512,128]{2,1,0:T(8,128)(2,1)S(1)}, u32[]{:S(2)}, u32[]{:S(2)}) collective-permute-start(bf16[4,512,128]{2,1,0:T(8,128)(2,1)} %bitcast.18), channel_id=1, source_target_pairs={{0,1},{1,2},{2,3},{4,5},{5,6},{6,7},{8,9},{9,10},{10,11},{12,13},{... | collective-permute-start | bytes 1572872 | tf_op jit(solution)/shard_map/ppermute | solution.py:300
  6.3 1.1 copy.17
  7.4 19.7 %all_to_all.10.got = bf16[32,64,128]{2,1,0:T(8,128)(2,1)S(1)} all-to-all(bf16[32,64,128]{2,1,0:T(8,128)(2,1)S(1)} %bitcast.22), channel_id=1, replica_groups={{0,4,8,12,16,20,24,28,128,132,136,140,144,148,152,156,256,260,264,268,2..., dimensions={0} | all-to-all | bytes 1048576 | tf_op jit(solution)/shard_map/all_to_all | solution.py:305
  27.1 0.0 collective-permute-done.1.after
  27.1 0.0 collective-permute-done.before
  27.1 0.0 copy-start.6
  27.1 0.8 copy-done.6
  27.9 1.1 arrange.1
  29.1 8.8 %collective-permute-start.2 = (bf16[8,128,128]{2,1,0:T(8,128)(2,1)S(1)}, bf16[8,128,128]{2,1,0:T(8,128)(2,1)}, u32[]{:S(2)}, u32[]{:S(2)}) collective-permute-start(bf16[8,128,128]{2,1,0:T(8,128)(2,1)S(1)} %get-tuple-element.15.a0), channel_id=1, source_target_pairs={{0,32},{4,36},{8,40},{12,44},{16,48},{20,52},{24,56},{28,60},{32,6... | collective-permute-start | bytes 786440 | tf_op jit(solution)/shard_map/ppermute | solution.py:310
  37.9 3.8 %collective-permute-start.5 = (bf16[8,128,128]{2,1,0:T(8,128)(2,1)}, bf16[8,128,128]{2,1,0:T(8,128)(2,1)}, u32[]{:S(2)}, u32[]{:S(2)}) collective-permute-start(bf16[8,128,128]{2,1,0:T(8,128)(2,1)} %get-tuple-element.16.b0), channel_id=1, source_target_pairs={{0,96},{4,100},{8,104},{12,108},{16,112},{20,116},{24,120},{28,124... | collective-permute-start | bytes 786440 | tf_op jit(solution)/shard_map/ppermute | solution.py:311
  41.6 7.3 %collective-permute-start.4 = (bf16[8,128,128]{2,1,0:T(8,128)(2,1)S(1)}, bf16[8,128,128]{2,1,0:T(8,128)(2,1)}, u32[]{:S(2)}, u32[]{:S(2)}) collective-permute-start(bf16[8,128,128]{2,1,0:T(8,128)(2,1)S(1)} %get-tuple-element.15.a0), channel_id=1, source_target_pairs={{0,96},{4,100},{8,104},{12,108},{16,112},{20,116},{24,120},{28,124... | collective-permute-start | bytes 786440 | tf_op jit(solution)/shard_map/ppermute | solution.py:313
  48.9 1.9 %collective-permute-start.3 = (bf16[8,128,128]{2,1,0:T(8,128)(2,1)}, bf16[8,128,128]{2,1,0:T(8,128)(2,1)}, u32[]{:S(2)}, u32[]{:S(2)}) collective-permute-start(bf16[8,128,128]{2,1,0:T(8,128)(2,1)} %get-tuple-element.16.b0), channel_id=1, source_target_pairs={{0,32},{4,36},{8,40},{12,44},{16,48},{20,52},{24,56},{28,60},{32,6... | collective-permute-start | bytes 786440 | tf_op jit(solution)/shard_map/ppermute | solution.py:312
  50.9 0.0 copy-done.12
  50.9 0.1 copy.14
  51.0 0.1 reshape.22.cols1
  51.1 0.0 copy-done.11
  51.1 0.1 copy.15
  51.2 0.1 reshape.23.cols2
  51.3 1.0 copy.16
  52.3 0.0 copy-done
  52.3 0.0 copy-start.4
  52.3 1.2 copy-done.4
  53.5 3.0 %factors.1 = (bf16[512,2048]{1,0:T(8,128)(2,1)S(1)}, bf16[512,512]{1,0:T(8,128)(2,1)S(1)}, bf16[2,4,128,128]{3,2,1,0:T(8,128)(2,1)S(1)}) custom-call(s32[64]{0:T(128)S(1)} %reshape.22.cols1, s32[160]{0:T(256)S(1)} %reshape.23.cols2, s32[1]{0:T(128)} %bitcast.own, bf16[2,8,4,64,64]{4,3,2,1,0:T(8,128)(2,1)S(1)} %copy-done.4, bf16[5,8,4,64,64]{4,3,2,1,0:T(8,128)(2,1)S(1)} %copy-done), custom_call_target="tpu_custom_call" | custom-call | flops 300000000 | bytes 8000000 | tf_op jit(solution)/shard_map/factors/pallas_call | solution.py:101
  56.5 0.0 copy-start.1
  56.5 1.3 copy-done.1
  57.8 0.0 copy-start.8
  57.8 0.8 copy-done.8
  58.6 23.5 %collective-permute-done.2.a3 = bf16[8,128,128]{2,1,0:T(8,128)(2,1)} collective-permute-done((bf16[8,128,128]{2,1,0:T(8,128)(2,1)S(1)}, bf16[8,128,128]{2,1,0:T(8,128)(2,1)}, u32[]{:S(2)}, u32[]{:S(2)}) %collective-permute-start.2) | collective-permute-done | bytes 262176 | tf_op jit(solution)/shard_map/ppermute | solution.py:310
  82.1 4.4 %collective-permute-start.6 = (bf16[8,128,128]{2,1,0:T(8,128)(2,1)}, bf16[8,128,128]{2,1,0:T(8,128)(2,1)S(1)}, u32[]{:S(2)}, u32[]{:S(2)}) collective-permute-start(bf16[8,128,128]{2,1,0:T(8,128)(2,1)} %collective-permute-done.2.a3), channel_id=1, source_target_pairs={{0,32},{4,36},{8,40},{12,44},{16,48},{20,52},{24,56},{28,60},{32,6... | collective-permute-start | bytes 786440 | tf_op jit(solution)/shard_map/ppermute | solution.py:314
  86.5 0.0 collective-permute-done.5.b1
  86.5 4.8 %collective-permute-start.7 = (bf16[8,128,128]{2,1,0:T(8,128)(2,1)}, bf16[8,128,128]{2,1,0:T(8,128)(2,1)S(1)}, u32[]{:S(2)}, u32[]{:S(2)}) collective-permute-start(bf16[8,128,128]{2,1,0:T(8,128)(2,1)} %collective-permute-done.5.b1), channel_id=1, source_target_pairs={{0,96},{4,100},{8,104},{12,108},{16,112},{20,116},{24,120},{28,124... | collective-permute-start | bytes 786440 | tf_op jit(solution)/shard_map/ppermute | solution.py:315
  91.3 0.0 collective-permute-done.4.a1
  91.3 0.9 collective-permute-done.3.b3
  92.2 3.6 %near.1.acc = f32[2,128,2048]{2,1,0:T(8,128)S(1)} custom-call(bf16[2,4,128,128]{3,2,1,0:T(8,128)(2,1)S(1)} %get-tuple-element.13.first, bf16[128,128]{1,0:T(8,128)(2,1)S(1)} %get-tuple-element.23.s3, bf16[8,128,128]{2,1,0:T(8,128)(2,1)S(1)} %get-tuple-element.15.a0, bf16[8,128,128]{2,1,0:T(8,128)(2,1)} %get-tuple-element.16.b0, ...), custom_call_target="tpu_custom_call" | custom-call | flops 800000000 | bytes 4000000 | tf_op jit(solution)/shard_map/near/pallas_call | solution.py:169
  95.8 0.0 copy-start.3
  95.8 0.0 copy-start.10
  95.8 2.0 %collective-permute-done.6.a2 = bf16[8,128,128]{2,1,0:T(8,128)(2,1)S(1)} collective-permute-done((bf16[8,128,128]{2,1,0:T(8,128)(2,1)}, bf16[8,128,128]{2,1,0:T(8,128)(2,1)S(1)}, u32[]{:S(2)}, u32[]{:S(2)}) %collective-permute-start.6) | collective-permute-done | bytes 262176 | tf_op jit(solution)/shard_map/ppermute | solution.py:314
  97.8 19.8 %collective-permute-done.7.b2 = bf16[8,128,128]{2,1,0:T(8,128)(2,1)S(1)} collective-permute-done((bf16[8,128,128]{2,1,0:T(8,128)(2,1)}, bf16[8,128,128]{2,1,0:T(8,128)(2,1)S(1)}, u32[]{:S(2)}, u32[]{:S(2)}) %collective-permute-start.7) | collective-permute-done | bytes 262176 | tf_op jit(solution)/shard_map/ppermute | solution.py:315
  117.6 2.7 %far.1 = bf16[32,2,64,128]{3,2,1,0:T(8,128)(2,1)} custom-call(bf16[2,4,128,128]{3,2,1,0:T(8,128)(2,1)S(1)} %get-tuple-element.13.first, bf16[128,128]{1,0:T(8,128)(2,1)S(1)} %get-tuple-element.23.s3, f32[2,128,2048]{2,1,0:T(8,128)S(1)} %near.1.acc, bf16[8,128,128]{2,1,0:T(8,128)(2,1)S(1)} %collective-permute-done.6.a2, ...), custom_call_target="tpu_custom_call" | custom-call | flops 400000000 | bytes 4000000 | tf_op jit(solution)/shard_map/far/pallas_call | solution.py:200
  120.3 4.1 %all-to-all-start.1 = ((bf16[32,128,128]{2,1,0:T(8,128)(2,1)}), bf16[32,128,128]{2,1,0:T(8,128)(2,1)S(1)}, u32[]{:S(2)}, u32[]{:S(2)}) async-start(bf16[32,128,128]{2,1,0:T(8,128)(2,1)} %bitcast.7), calls=%async_computation.1 | async-start | bytes 2097152 | tf_op jit(solution)/shard_map/all_to_all | solution.py:329
  125.1 0.0 copy-done.3
  125.1 0.0 copy-done.10
  125.1 0.0 copy-start.2
  125.1 1.6 %copy-done.2 = bf16[512,2048]{1,0:T(8,128)(2,1)S(1)} copy-done((bf16[512,2048]{1,0:T(8,128)(2,1)S(1)}, bf16[512,2048]{1,0:T(8,128)(2,1)}, u32[]{:S(2)}) %copy-start.2) | copy-done | bytes 2097176
  126.7 0.0 copy-start.7
  126.7 1.0 copy-done.7
  127.7 3.9 %local_terms.1.base = f32[4,512,128]{2,1,0:T(8,128)S(1)} custom-call(s32[3]{0:T(128)S(1)} %copy-done.10, bf16[512,2048]{1,0:T(8,128)(2,1)S(1)} %copy-done.2, bf16[128,128]{1,0:T(8,128)(2,1)S(1)} %get-tuple-element.22.r3, bf16[4,512,128]{2,1,0:T(8,128)(2,1)S(1)} %bitcast.20, bf16[4,512,128]{2,1,0:T(8,128)(2,1)S(1)} %copy-done.7, ...), custom_call_target="tpu_custom_call" | custom-call | flops 1200000000 | bytes 5000000 | tf_op jit(solution)/shard_map/local_terms/pallas_call | solution.py:234
  131.6 9.8 %all-to-all-done.1 = bf16[32,128,128]{2,1,0:T(8,128)(2,1)S(1)} async-done(((bf16[32,128,128]{2,1,0:T(8,128)(2,1)}), bf16[32,128,128]{2,1,0:T(8,128)(2,1)S(1)}, u32[]{:S(2)}, u32[]{:S(2)}) %all-to-all-start.1) | async-done | bytes 1048608 | tf_op jit(solution)/shard_map/all_to_all | solution.py:329
  141.4 0.0 copy-start.5
  141.4 1.2 copy-done.5
  142.7 0.0 copy-start.9
  142.7 1.0 copy-done.9
  143.7 2.5 %finish.1 = (bf16[4,512,128]{2,1,0:T(8,128)(2,1)}, f32[4,512,128]{2,1,0:T(8,128)}) custom-call(f32[1]{0:T(128)S(6)} %copy.18.weight, bf16[512,512]{1,0:T(8,128)(2,1)S(1)} %copy-done.9, bf16[32,2,4,16,128]{4,3,2,1,0:T(8,128)(2,1)S(1)} %bitcast.16, f32[4,512,128]{2,1,0:T(8,128)S(1)} %local_terms.1.base, f32[4,512,128]{2,1,0:T(8,128)S(1)} %bitcast.21), custom_call_target="tpu_custom_call" | custom-call | flops 300000000 | bytes 6000000 | tf_op jit(solution)/shard_map/finish/pallas_call | solution.py:264
  (1 shorter events, 0.0 us)
Async XLA Ops:
  0.6 50.3 %copy-start.12 = (s32[2,8,4]{1,2,0:T(4,128)S(1)}, s32[2,8,4]{1,2,0:T(4,128)}, u32[]{:S(2)}) copy-start(s32[2,8,4]{1,2,0:T(4,128)} %param.13) | copy-start | bytes 772
  0.6 50.4 %copy-start.11 = (s32[5,8,4]{1,2,0:T(4,128)S(1)}, s32[5,8,4]{1,2,0:T(4,128)}, u32[]{:S(2)}) copy-start(s32[5,8,4]{1,2,0:T(4,128)} %param.15) | copy-start | bytes 1924
  0.7 51.6 %copy-start = (bf16[5,8,4,64,64]{4,3,2,1,0:T(8,128)(2,1)S(1)}, bf16[5,8,4,64,64]{4,3,2,1,0:T(8,128)(2,1)}, u32[]{:S(2)}) copy-start(bf16[5,8,4,64,64]{4,3,2,1,0:T(8,128)(2,1)} %b2.1) | copy-start | bytes 3932164
  0.7 26.5 %collective-permute-start.1 = (bf16[4,512,128]{2,1,0:T(8,128)(2,1)}, bf16[4,512,128]{2,1,0:T(8,128)(2,1)S(1)}, u32[]{:S(2)}, u32[]{:S(2)}) collective-permute-start(bf16[4,512,128]{2,1,0:T(8,128)(2,1)} %bitcast.17), channel_id=1, source_target_pairs={{1,0},{2,1},{3,2},{5,4},{6,5},{7,6},{9,8},{10,9},{11,10},{13,12},{... | collective-permute-start | bytes 1572872 | tf_op jit(solution)/shard_map/ppermute | solution.py:301
  2.9 24.3 %collective-permute-start = (bf16[4,512,128]{2,1,0:T(8,128)(2,1)}, bf16[4,512,128]{2,1,0:T(8,128)(2,1)S(1)}, u32[]{:S(2)}, u32[]{:S(2)}) collective-permute-start(bf16[4,512,128]{2,1,0:T(8,128)(2,1)} %bitcast.18), channel_id=1, source_target_pairs={{0,1},{1,2},{2,3},{4,5},{5,6},{6,7},{8,9},{9,10},{10,11},{12,13},{... | collective-permute-start | bytes 1572872 | tf_op jit(solution)/shard_map/ppermute | solution.py:300
  27.1 0.8 copy-start.6
  29.1 53.0 %collective-permute-start.2 = (bf16[8,128,128]{2,1,0:T(8,128)(2,1)S(1)}, bf16[8,128,128]{2,1,0:T(8,128)(2,1)}, u32[]{:S(2)}, u32[]{:S(2)}) collective-permute-start(bf16[8,128,128]{2,1,0:T(8,128)(2,1)S(1)} %get-tuple-element.15.a0), channel_id=1, source_target_pairs={{0,32},{4,36},{8,40},{12,44},{16,48},{20,52},{24,56},{28,60},{32,6... | collective-permute-start | bytes 786440 | tf_op jit(solution)/shard_map/ppermute | solution.py:310
  37.9 48.6 %collective-permute-start.5 = (bf16[8,128,128]{2,1,0:T(8,128)(2,1)}, bf16[8,128,128]{2,1,0:T(8,128)(2,1)}, u32[]{:S(2)}, u32[]{:S(2)}) collective-permute-start(bf16[8,128,128]{2,1,0:T(8,128)(2,1)} %get-tuple-element.16.b0), channel_id=1, source_target_pairs={{0,96},{4,100},{8,104},{12,108},{16,112},{20,116},{24,120},{28,124... | collective-permute-start | bytes 786440 | tf_op jit(solution)/shard_map/ppermute | solution.py:311
  41.6 49.7 %collective-permute-start.4 = (bf16[8,128,128]{2,1,0:T(8,128)(2,1)S(1)}, bf16[8,128,128]{2,1,0:T(8,128)(2,1)}, u32[]{:S(2)}, u32[]{:S(2)}) collective-permute-start(bf16[8,128,128]{2,1,0:T(8,128)(2,1)S(1)} %get-tuple-element.15.a0), channel_id=1, source_target_pairs={{0,96},{4,100},{8,104},{12,108},{16,112},{20,116},{24,120},{28,124... | collective-permute-start | bytes 786440 | tf_op jit(solution)/shard_map/ppermute | solution.py:313
  48.9 43.3 %collective-permute-start.3 = (bf16[8,128,128]{2,1,0:T(8,128)(2,1)}, bf16[8,128,128]{2,1,0:T(8,128)(2,1)}, u32[]{:S(2)}, u32[]{:S(2)}) collective-permute-start(bf16[8,128,128]{2,1,0:T(8,128)(2,1)} %get-tuple-element.16.b0), channel_id=1, source_target_pairs={{0,32},{4,36},{8,40},{12,44},{16,48},{20,52},{24,56},{28,60},{32,6... | collective-permute-start | bytes 786440 | tf_op jit(solution)/shard_map/ppermute | solution.py:312
  52.3 1.2 copy-start.4
  56.5 1.3 copy-start.1
  57.8 0.8 copy-start.8
  82.1 15.7 %collective-permute-start.6 = (bf16[8,128,128]{2,1,0:T(8,128)(2,1)}, bf16[8,128,128]{2,1,0:T(8,128)(2,1)S(1)}, u32[]{:S(2)}, u32[]{:S(2)}) collective-permute-start(bf16[8,128,128]{2,1,0:T(8,128)(2,1)} %collective-permute-done.2.a3), channel_id=1, source_target_pairs={{0,32},{4,36},{8,40},{12,44},{16,48},{20,52},{24,56},{28,60},{32,6... | collective-permute-start | bytes 786440 | tf_op jit(solution)/shard_map/ppermute | solution.py:314
  86.5 31.1 %collective-permute-start.7 = (bf16[8,128,128]{2,1,0:T(8,128)(2,1)}, bf16[8,128,128]{2,1,0:T(8,128)(2,1)S(1)}, u32[]{:S(2)}, u32[]{:S(2)}) collective-permute-start(bf16[8,128,128]{2,1,0:T(8,128)(2,1)} %collective-permute-done.5.b1), channel_id=1, source_target_pairs={{0,96},{4,100},{8,104},{12,108},{16,112},{20,116},{24,120},{28,124... | collective-permute-start | bytes 786440 | tf_op jit(solution)/shard_map/ppermute | solution.py:315
  95.8 29.3 %copy-start.3 = (bf16[1,4,512,128]{3,2,1,0:T(8,128)(2,1)S(1)}, bf16[1,4,512,128]{3,2,1,0:T(8,128)(2,1)}, u32[]{:S(2)}) copy-start(bf16[1,4,512,128]{3,2,1,0:T(8,128)(2,1)} %param.9) | copy-start | bytes 1572868
  95.8 29.3 %copy-start.10 = (s32[3]{0:T(128)S(1)}, s32[3]{0:T(128)}, u32[]{:S(2)}) copy-start(s32[3]{0:T(128)} %offsets.1) | copy-start | bytes 40
  120.3 21.1 %all-to-all-start.1 = ((bf16[32,128,128]{2,1,0:T(8,128)(2,1)}), bf16[32,128,128]{2,1,0:T(8,128)(2,1)S(1)}, u32[]{:S(2)}, u32[]{:S(2)}) async-start(bf16[32,128,128]{2,1,0:T(8,128)(2,1)} %bitcast.7), calls=%async_computation.1 | async-start | bytes 2097152 | tf_op jit(solution)/shard_map/all_to_all | solution.py:329
  125.1 1.6 %copy-start.2 = (bf16[512,2048]{1,0:T(8,128)(2,1)S(1)}, bf16[512,2048]{1,0:T(8,128)(2,1)}, u32[]{:S(2)}) copy-start(bf16[512,2048]{1,0:T(8,128)(2,1)} %copy-done.1) | copy-start | bytes 6291460
  126.7 1.0 copy-start.7
  141.4 1.2 copy-start.5
  142.7 1.0 copy-start.9

commit v2 on v1

v2 whole, which is shorter than its diff:
```python
import functools

import jax
import jax.numpy as jnp
from jax import lax
from jax.experimental import pallas as pl
from jax.experimental.pallas import tpu as pltpu
from jax.sharding import PartitionSpec as P

NX, NZ, NY, NC = 4, 4, 4, 2
PLANE = NX * NY * NC
BF = jnp.bfloat16
F32 = jnp.float32


def row_of(x, z, y, core):
    return ((x * NZ + z % NZ) * NY + y) * NC + core


def plane_groups():
    return [
        [row_of(x, z, y, c) for x in range(NX) for y in range(NY) for c in range(NC)]
        for z in range(NZ)
    ]


def z_swap(sign):
    return [
        (row_of(x, z, y, c), row_of(x, z + (sign if (z + c) % 2 == 0 else -sign), y, c))
        for x in range(NX)
        for z in range(NZ)
        for y in range(NY)
        for c in range(NC)
    ]


def place_of(row):
    z, core = (row >> 3) & 3, row & 1
    step = 1 - 2 * ((z + core) & 1)
    return z, step, half_of(z, core)


def half_of(z, core):
    return ((z + 1 - core) >> 1) & 1


def cost(flops, moved):
    return pl.CostEstimate(flops=flops, bytes_accessed=moved, transcendentals=0)


SMALL = pltpu.CompilerParams(vmem_limit_bytes=24 * 1024 * 1024)


def iota2(shape):
    return (
        lax.broadcasted_iota(jnp.int32, shape, 0),
        lax.broadcasted_iota(jnp.int32, shape, 1),
    )


def onehot(rows_match):
    return jnp.where(rows_match, 1.0, 0.0).astype(BF)


def dot(a, b):
    return jnp.dot(a, b, preferred_element_type=F32)


def factors_kernel(cols1, cols2, row_ref, b1, b2, second, sync2, first, dense):
    second[...] = jnp.zeros_like(second)
    sync2[...] = jnp.zeros_like(sync2)
    dense[...] = jnp.zeros_like(dense)

    def place(dst, r, base, c, blk):
        zero = jnp.zeros_like(blk)
        left = jnp.concatenate([blk, zero], axis=1)
        right = jnp.concatenate([zero, blk], axis=1)
        wide = jnp.where((c & 1) == 0, left, right)
        at = (
            pl.ds(pl.multiple_of(r * 64, 64), 64),
            pl.ds(pl.multiple_of(base + (c >> 1) * 128, 128), 128),
        )
        dst[at] = dst[at] + wide

    def row(r, carry):
        for k in range(4):
            for t in range(2):
                place(dense.at[t], r, 0, cols1[t * 32 + r * 4 + k], b1[t, r, k])
            place(sync2, r, 0, cols2[32 + r * 4 + k], b2[1, r, k])
            for t, base in ((0, 0), (2, 512), (3, 1024), (4, 1536)):
                place(second, r, base, cols2[t * 32 + r * 4 + k], b2[t, r, k])
        return carry

    lax.fori_loop(0, 8, row, 0)
    me, step, _ = place_of(row_ref[0])
    i, j = iota2((512, 512))
    source = ((j >> 5) & 3) * 128 + (j >> 7) * 32 + (j & 31)
    swap = onehot(i == source)
    for d in range(2):
        at = (me + d * step) & 3
        for t in range(2):
            rows = jnp.concatenate(
                [dense[t, pl.ds(pl.multiple_of(x * 128 + at * 32, 32), 32), :] for x in range(4)],
                axis=0,
            )
            turned = dot(rows, swap).astype(BF)
            for z in range(4):
                first[d, t, ((z - me) * step) & 3] = turned[:, z * 128 : (z + 1) * 128]


def factors(cols1, cols2, row, b1, b2):
    smem = pl.BlockSpec(memory_space=pltpu.SMEM)
    vmem = pl.BlockSpec(memory_space=pltpu.VMEM)
    return pl.pallas_call(
        factors_kernel,
        out_shape=(
            jax.ShapeDtypeStruct((512, 2048), BF),
            jax.ShapeDtypeStruct((512, 512), BF),
            jax.ShapeDtypeStruct((2, 2, 4, 128, 128), BF),
        ),
        in_specs=[smem, smem, smem, vmem, vmem],
        out_specs=(vmem, vmem, vmem),
        scratch_shapes=[pltpu.VMEM((2, 512, 512), BF)],
        cost_estimate=cost(300_000_000, 8_000_000),
        compiler_params=SMALL,
        name="factors",
    )(cols1, cols2, row, b1, b2)


def arrange_kernel(row_ref, got, mine, other):
    _, _, half = place_of(row_ref[0])
    i, j = iota2((256, 256))
    move = onehot(j == ((i >> 2) & 3) * 64 + (i & 3) * 16 + (i >> 4))
    for g in range(8):
        block = got[4 * g : 4 * g + 4].reshape(256, 128)
        out = dot(move, block)
        at = slice(g * 16, g * 16 + 16)
        for m in range(8):
            low = out[m * 16 : m * 16 + 16, :]
            high = out[m * 16 + 128 : m * 16 + 144, :]
            mine[m, at, :] = jnp.where(half == 0, low, high).astype(BF)
            other[m, at, :] = jnp.where(half == 0, high, low).astype(BF)


def arrange(row, got):
    one = jax.ShapeDtypeStruct((8, 128, 128), BF)
    return pl.pallas_call(
        arrange_kernel,
        out_shape=(one, one),
        in_specs=[pl.BlockSpec(memory_space=pltpu.SMEM), pl.BlockSpec(memory_space=pltpu.VMEM)],
        cost_estimate=cost(130_000_000, 1_100_000),
        compiler_params=SMALL,
        name="arrange",
    )(row, got)


def twice(s3):
    zero = jnp.zeros_like(s3)
    return jnp.concatenate(
        [jnp.concatenate([s3, zero], axis=1), jnp.concatenate([zero, s3], axis=1)], axis=0
    )


def near_kernel(first, s3, mine, pair, cross, acc):
    s3_twice = twice(s3[...])
    for p in range(4):
        sums = [[None, None], [None, None]]
        for slot, part in ((0, mine), (1, pair), (3, cross)):
            x = jnp.concatenate([part[2 * p], part[2 * p + 1]], axis=1)
            inputs = (x, dot(x, s3_twice).astype(BF))
            for d in range(2):
                for t in range(2):
                    got = dot(first[d, t, slot], inputs[t])
                    sums[d][t] = got if sums[d][t] is None else sums[d][t] + got
        for d in range(2):
            for t in range(2):
                acc[d, t, :, p * 256 : p * 256 + 256] = sums[d][t]


def near(first, s3, mine, pair, cross):
    return pl.pallas_call(
        near_kernel,
        out_shape=jax.ShapeDtypeStruct((2, 2, 128, 1024), F32),
        cost_estimate=cost(700_000_000, 4_000_000),
        compiler_params=SMALL,
        name="near",
    )(first, s3, mine, pair, cross)


def far_kernel(d, first, s3, acc, part, out, keep):
    s3_twice = twice(s3[...])
    for p in range(4):
        at = slice(p * 256, p * 256 + 256)
        x = jnp.concatenate([part[2 * p], part[2 * p + 1]], axis=1)
        inputs = (x, dot(x, s3_twice).astype(BF))
        for t in range(2):
            keep[t, :, at] = (acc[d, t, :, at] + dot(first[d, t, 2], inputs[t])).astype(BF)
    i, j = iota2((128, 128))
    move = onehot(i == ((j >> 2) & 3) * 32 + (j & 3) * 8 + (j >> 4))
    for t in range(2):
        for g in range(8):
            rows = jnp.concatenate(
                [keep[t, g * 16 : g * 16 + 16, m * 128 : m * 128 + 128] for m in range(8)],
                axis=0,
            )
            out[4 * g : 4 * g + 4, t] = dot(move, rows).astype(BF).reshape(4, 32, 128)


def far(d, first, s3, acc, part):
    return pl.pallas_call(
        functools.partial(far_kernel, d),
        out_shape=jax.ShapeDtypeStruct((32, 2, 32, 128), BF),
        scratch_shapes=[pltpu.VMEM((2, 128, 1024), BF)],
        cost_estimate=cost(200_000_000, 2_000_000),
        compiler_params=SMALL,
        name="far",
    )(first, s3, acc, part)


def local_kernel(offsets, second, r3, state, before, after, out, stack):
    x = state[0]
    stack[0:512, :] = x
    for k in range(3):
        off = offsets[k]
        rows = slice(512 * (k + 1), 512 * (k + 2))

        @pl.when(off == 1)
        def _():
            stack[rows, :] = before[0]

        @pl.when(off == 0)
        def _():
            stack[rows, :] = state[0]

        @pl.when(off == -1)
        def _():
            stack[rows, :] = after[0]

    out[0] = x.astype(F32) + dot(x, r3[...]) + dot(second[...], stack[...])


def local_terms(offsets, second, r3, state, before, after):
    slab = pl.BlockSpec((1, 512, 128), lambda b: (b, 0, 0))
    return pl.pallas_call(
        local_kernel,
        grid=(4,),
        out_shape=jax.ShapeDtypeStruct((4, 512, 128), F32),
        in_specs=[
            pl.BlockSpec(memory_space=pltpu.SMEM),
            pl.BlockSpec((512, 2048), lambda b: (0, 0)),
            pl.BlockSpec((128, 128), lambda b: (0, 0)),
            slab,
            slab,
            slab,
        ],
        out_specs=slab,
        scratch_shapes=[pltpu.VMEM((2048, 128), BF)],
        cost_estimate=cost(1_200_000_000, 5_000_000),
        compiler_params=SMALL,
        name="local_terms",
    )(offsets, second, r3, state, before, after)


def finish_kernel(weight, row_ref, sync2, back1, back2, base, accum, state_out, accum_out):
    z, _, _ = place_of(row_ref[0])
    core = lax.broadcasted_iota(jnp.int32, (PLANE, 8, 128), 0) & 1
    low_first = jnp.where(core == 0, half_of(z, 0), half_of(z, 1)) == 0

    def joined(t):
        one, two = back1[:, t, 0].astype(F32), back2[:, t, 0].astype(F32)
        parts = [jnp.where(low_first, one, two), jnp.where(low_first, two, one)]
        return jnp.concatenate(parts, axis=1).reshape(512, 128)

    total = base[0] + joined(0) + dot(sync2[...], joined(1).astype(BF))
    state_out[0] = total.astype(BF)
    accum_out[0] = accum[0] + weight[0] * total


def finish(weight, row, sync2, back1, back2, base, accum):
    slab = pl.BlockSpec((1, 512, 128), lambda b: (b, 0, 0))
    part = pl.BlockSpec((32, 2, 1, 8, 128), lambda b: (0, 0, b, 0, 0))
    smem = pl.BlockSpec(memory_space=pltpu.SMEM)
    return pl.pallas_call(
        finish_kernel,
        grid=(4,),
        out_shape=(
            jax.ShapeDtypeStruct((4, 512, 128), BF),
            jax.ShapeDtypeStruct((4, 512, 128), F32),
        ),
        in_specs=[smem, smem, pl.BlockSpec((512, 512), lambda b: (0, 0)), part, part, slab, slab],
        out_specs=(slab, slab),
        cost_estimate=cost(300_000_000, 6_000_000),
        compiler_params=SMALL,
        name="finish",
    )(weight, row, sync2, back1, back2, base, accum)


def local(
    state,
    accum,
    poisson_weight,
    route1_blocks,
    route1_cols,
    route2_blocks,
    route2_cols,
    route3_factors,
    fleet_offsets,
):
    field = state[0]
    levels = lax.axis_size("col")
    up = [(i, i + 1) for i in range(levels - 1)]
    down = [(i + 1, i) for i in range(levels - 1)]
    before = lax.ppermute(field, "col", up)
    after = lax.ppermute(field, "col", down)
    groups = plane_groups()

    split = field.reshape(4, PLANE, 16, 128).transpose(1, 0, 2, 3).reshape(PLANE, 64, 128)
    got = lax.all_to_all(split, "row", 0, 0, tiled=True, axis_index_groups=groups)
    got, before, after = lax.optimization_barrier((got, before, after))
    row = lax.axis_index("row").astype(jnp.int32).reshape(1)
    mine, other = arrange(row, got)

    swap, across = z_swap(1), z_swap(-1)
    pair = lax.ppermute(other, "row", swap)
    opposite = lax.ppermute(pair, "row", across)

    second, sync2, first = factors(
        route1_cols.reshape(-1),
        route2_cols.reshape(-1),
        row,
        route1_blocks,
        route2_blocks,
    )
    ready, first = lax.optimization_barrier((mine, first))
    cross = lax.ppermute(ready, "row", across)
    turned = jnp.swapaxes(route3_factors, 1, 2)
    base = local_terms(fleet_offsets, second, turned[0], field, before, after)
    acc = near(first, turned[1], mine, pair, cross)
    acc, base, opposite = lax.optimization_barrier((acc, base, opposite))
    theirs = far(1, first, turned[1], acc, opposite)
    ours = far(0, first, turned[1], acc, opposite)
    swapped = lax.ppermute(theirs, "row", swap)

    def collect(value):
        value = value.reshape(PLANE, 64, 128)
        back = lax.all_to_all(value, "row", 0, 0, tiled=True, axis_index_groups=groups)
        return back.reshape(PLANE, 2, 4, 8, 128)

    state_out, accum_out = finish(
        poisson_weight, row, sync2, collect(ours), collect(swapped), base, accum[0]
    )
    return state_out[None], accum_out[None]


def solution(mesh):
    placed = (
        P("col", "row", None, None),
        P("col", "row", None, None),
        P(),
        P(),
        P(),
        P(),
        P(),
        P(),
        P(),
    )
    return jax.shard_map(
        local,
        mesh=mesh,
        in_specs=placed,
        out_specs=(P("col", "row", None, None), P("col", "row", None, None)),
        check_vma=False,
    )
```

time: 147 us -> 136 us (0.925)
  the two profiles are of different devices: /device:TPU:65 before, /device:TPU:33 now
where the time goes in v2:
time: 136 us; the launch traced here: 135 us
  starting transfers between devices  49.8 us (37%)
  waiting for transfers between devices  36.7 us (27%)
  blocking collectives  24.8 us (18%)
  Pallas kernels  15.7 us (12%)
  local copies, waits for them, and re-layouts  6.34 us (5%)
  between operations  1.51 us (1%)
    all_to_all x1, blocking collectives, collect(): lax.all_to_all(value, 'row', 0, 0, tiled=True, axis_index_groups=groups)  24.8 us
    ppermute x1, waiting for transfers between devices, local(): opposite = lax.ppermute(pair, 'row', across)  12.9 us
    all_to_all x1, starting transfers between devices, collect(): lax.all_to_all(value, 'row', 0, 0, tiled=True, axis_index_groups=groups)  11.7 us
    all_to_all x1, waiting for transfers between devices, local(): lax.all_to_all(split, 'row', 0, 0, tiled=True, axis_index_groups=groups)  11.7 us
    ppermute x1, starting transfers between devices, local(): pair = lax.ppermute(other, 'row', swap)  11.6 us
    all_to_all x1, waiting for transfers between devices, collect(): lax.all_to_all(value, 'row', 0, 0, tiled=True, axis_index_groups=groups)  11 us
    all_to_all x1, starting transfers between devices, local(): lax.all_to_all(split, 'row', 0, 0, tiled=True, axis_index_groups=groups)  8.14 us
    ppermute x1, starting transfers between devices, local(): cross = lax.ppermute(ready, 'row', across)  5.18 us
  transfers between devices with their start and end apart: 8, of which 4 were waited for; matrix products, arithmetic and copies ran while one was open for 2% of the time, Pallas kernels for 8%

profile of v2, /device:TPU:33, one launch (start us, length us, event | category | flops | bytes accessed | tf_op | source)
XLA Modules:
  0.0 134.8 jit_solution(17004380967497607907)
XLA Ops:
  0.6 0.0 copy-start.9
  0.6 0.0 copy-start.8
  0.7 0.0 copy-start
  0.7 2.2 %collective-permute-start.1 = (bf16[4,512,128]{2,1,0:T(8,128)(2,1)}, bf16[4,512,128]{2,1,0:T(8,128)(2,1)}, u32[]{:S(2)}, u32[]{:S(2)}) collective-permute-start(bf16[4,512,128]{2,1,0:T(8,128)(2,1)} %bitcast.18), channel_id=1, source_target_pairs={{1,0},{2,1},{3,2},{5,4},{6,5},{7,6},{9,8},{10,9},{11,10},{13,12},{... | collective-permute-start | bytes 1572872 | tf_op jit(solution)/shard_map/ppermute | solution.py:314
  2.9 3.5 %collective-permute-start = (bf16[4,512,128]{2,1,0:T(8,128)(2,1)}, bf16[4,512,128]{2,1,0:T(8,128)(2,1)}, u32[]{:S(2)}, u32[]{:S(2)}) collective-permute-start(bf16[4,512,128]{2,1,0:T(8,128)(2,1)} %bitcast.19), channel_id=1, source_target_pairs={{0,1},{1,2},{2,3},{4,5},{5,6},{6,7},{8,9},{9,10},{10,11},{12,13},{... | collective-permute-start | bytes 1572872 | tf_op jit(solution)/shard_map/ppermute | solution.py:313
  6.4 1.9 %copy.16 = bf16[4,32,16,128]{3,2,0,1:T(8,128)(2,1)} copy(bf16[4,32,16,128]{3,2,1,0:T(8,128)(2,1)} %bitcast.20) | data formatting | bytes 1048576 | tf_op jit(solution)/shard_map/reshape;squeeze | solution.py:317
  8.3 8.1 %all-to-all-start = ((bf16[32,64,128]{2,1,0:T(8,128)(2,1)}), bf16[32,64,128]{2,1,0:T(8,128)(2,1)S(1)}, u32[]{:S(2)}, u32[]{:S(2)}) async-start(bf16[32,64,128]{2,1,0:T(8,128)(2,1)} %bitcast.26), calls=%async_computation | async-start | bytes 1048576 | tf_op jit(solution)/shard_map/all_to_all | solution.py:318
  16.5 11.7 %all-to-all-done.got = bf16[32,64,128]{2,1,0:T(8,128)(2,1)S(1)} async-done(((bf16[32,64,128]{2,1,0:T(8,128)(2,1)}), bf16[32,64,128]{2,1,0:T(8,128)(2,1)S(1)}, u32[]{:S(2)}, u32[]{:S(2)}) %all-to-all-start) | async-done | bytes 524320 | tf_op jit(solution)/shard_map/all_to_all | solution.py:318
  28.1 0.0 collective-permute-done.1.after
  28.1 0.0 collective-permute-done.before
  28.1 0.0 copy-start.6
  28.1 1.1 arrange.1
  29.3 0.0 copy-start.1
  29.3 11.6 %collective-permute-start.2 = (bf16[8,128,128]{2,1,0:T(8,128)(2,1)}, bf16[8,128,128]{2,1,0:T(8,128)(2,1)}, u32[]{:S(2)}, u32[]{:S(2)}) collective-permute-start(bf16[8,128,128]{2,1,0:T(8,128)(2,1)} %get-tuple-element.22), channel_id=1, source_target_pairs={{0,32},{4,100},{8,40},{12,108},{16,48},{20,116},{24,56},{28,124},{... | collective-permute-start | bytes 786440 | tf_op jit(solution)/shard_map/ppermute | solution.py:324
  40.9 0.0 copy-done.9
  40.9 0.1 copy.14
  41.0 0.1 reshape.29.cols1
  41.1 0.0 copy-done.8
  41.1 0.1 copy.15
  41.2 0.1 reshape.30.cols2
  41.3 1.0 copy.17
  42.3 0.0 copy-done
  42.3 0.0 copy-start.2
  42.3 1.2 copy-done.2
  43.5 3.0 %factors.1 = (bf16[512,2048]{1,0:T(8,128)(2,1)S(1)}, bf16[512,512]{1,0:T(8,128)(2,1)S(1)}, bf16[2,2,4,128,128]{4,3,2,1,0:T(8,128)(2,1)S(1)}) custom-call(s32[64]{0:T(128)S(1)} %reshape.29.cols1, s32[160]{0:T(256)S(1)} %reshape.30.cols2, s32[1]{0:T(128)} %bitcast.row_ref, bf16[2,8,4,64,64]{4,3,2,1,0:T(8,128)(2,1)S(1)} %copy-done.2, ...), custom_call_target="tpu_custom_call" | custom-call | flops 300000000 | bytes 8000000 | tf_op jit(solution)/shard_map/factors/pallas_call | solution.py:114
  46.6 0.0 copy-start.4
  46.6 5.2 %collective-permute-start.3 = (bf16[8,128,128]{2,1,0:T(8,128)(2,1)S(1)}, bf16[8,128,128]{2,1,0:T(8,128)(2,1)S(1)}, u32[]{:S(2)}, u32[]{:S(2)}) collective-permute-start(bf16[8,128,128]{2,1,0:T(8,128)(2,1)S(1)} %get-tuple-element.23.mine), channel_id=1, source_target_pairs={{0,96},{4,36},{8,104},{12,44},{16,112},{20,52},{24,120},{28,60},{3... | collective-permute-start | bytes 786440 | tf_op jit(solution)/shard_map/ppermute | solution.py:335
  51.8 1.1 collective-permute-done.2.pair
  52.9 3.0 %collective-permute-start.4 = (bf16[8,128,128]{2,1,0:T(8,128)(2,1)}, bf16[8,128,128]{2,1,0:T(8,128)(2,1)S(1)}, u32[]{:S(2)}, u32[]{:S(2)}) collective-permute-start(bf16[8,128,128]{2,1,0:T(8,128)(2,1)} %collective-permute-done.2.pair), channel_id=1, source_target_pairs={{0,96},{4,36},{8,104},{12,44},{16,112},{20,52},{24,120},{28,60},{3... | collective-permute-start | bytes 786440 | tf_op jit(solution)/shard_map/ppermute | solution.py:325
  55.9 0.0 copy-done.6
  55.9 0.0 copy-done.1
  55.9 4.5 %local_terms.1.base = f32[4,512,128]{2,1,0:T(8,128)S(1)} custom-call(s32[3]{0:T(128)S(1)} %copy-done.6, bf16[512,2048]{1,0:T(8,128)(2,1)S(1)} %get-tuple-element.24.second, bf16[128,128]{1,0:T(8,128)(2,1)S(1)} %get-tuple-element.32.r3, bf16[4,512,128]{2,1,0:T(8,128)(2,1)S(1)} %bitcast.21, bf16[4,512,128]{2,1,0:T(8,128)(2,1)} %collective-permute-done.before, ...), custom_call_target="tpu_custom_call" | custom-call | flops 1200000000 | bytes 5000000 | tf_op jit(solution)/shard_map/local_terms/pallas_call | solution.py:244
  60.5 0.0 copy-done.4
  60.5 0.0 collective-permute-done.3.cross
  60.5 2.7 %near.1.acc = f32[2,2,128,1024]{3,2,1,0:T(8,128)S(1)} custom-call(bf16[2,2,4,128,128]{4,3,2,1,0:T(8,128)(2,1)S(1)} %get-tuple-element.21.first, bf16[128,128]{1,0:T(8,128)(2,1)S(1)} %get-tuple-element.33.s3, bf16[8,128,128]{2,1,0:T(8,128)(2,1)S(1)} %get-tuple-element.23.mine, bf16[8,128,128]{2,1,0:T(8,128)(2,1)} %collective-permute-done.2.pair, ...), custom_call_target="tpu_custom_call" | custom-call | flops 700000000 | bytes 4000000 | tf_op jit(solution)/shard_map/near/pallas_call | solution.py:181
  63.2 12.9 %collective-permute-done.4.part = bf16[8,128,128]{2,1,0:T(8,128)(2,1)S(1)} collective-permute-done((bf16[8,128,128]{2,1,0:T(8,128)(2,1)}, bf16[8,128,128]{2,1,0:T(8,128)(2,1)S(1)}, u32[]{:S(2)}, u32[]{:S(2)}) %collective-permute-start.4) | collective-permute-done | bytes 262176 | tf_op jit(solution)/shard_map/ppermute | solution.py:325
  76.1 0.9 far.3
  77.0 0.0 copy-start.3
  77.0 4.4 %collective-permute-start.5 = (bf16[32,2,32,128]{3,2,1,0:T(8,128)(2,1)S(1)}, bf16[32,2,32,128]{3,2,1,0:T(8,128)(2,1)S(1)}, u32[]{:S(2)}, u32[]{:S(2)}) collective-permute-start(bf16[32,2,32,128]{3,2,1,0:T(8,128)(2,1)S(1)} %far.3), channel_id=1, source_target_pairs={{0,32},{4,100},{8,40},{12,108},{16,48},{20,116},{24,56},{28,124},{... | collective-permute-start | bytes 1572872 | tf_op jit(solution)/shard_map/ppermute | solution.py:342
  81.4 0.9 far.2
  82.3 24.8 %all_to_all.15 = bf16[32,64,128]{2,1,0:T(8,128)(2,1)S(1)} all-to-all(bf16[32,64,128]{2,1,0:T(8,128)(2,1)S(1)} %bitcast.24), channel_id=1, replica_groups={{0,4,8,12,16,20,24,28,128,132,136,140,144,148,152,156,256,260,264,268,2..., dimensions={0} | all-to-all | bytes 1048576 | tf_op jit(solution)/shard_map/all_to_all | solution.py:346
  107.1 0.0 collective-permute-done.5
  107.1 0.0 copy-start.7
  107.1 0.8 copy-done.7
  107.9 11.7 %all-to-all-start.2 = ((bf16[32,64,128]{2,1,0:T(8,128)(2,1)}), bf16[32,64,128]{2,1,0:T(8,128)(2,1)S(1)}, u32[]{:S(2)}, u32[]{:S(2)}) async-start(bf16[32,64,128]{2,1,0:T(8,128)(2,1)} %bitcast.27), calls=%async_computation.2 | async-start | bytes 1048576 | tf_op jit(solution)/shard_map/all_to_all | solution.py:346
  120.2 11.0 %all-to-all-done.2 = bf16[32,64,128]{2,1,0:T(8,128)(2,1)S(1)} async-done(((bf16[32,64,128]{2,1,0:T(8,128)(2,1)}), bf16[32,64,128]{2,1,0:T(8,128)(2,1)S(1)}, u32[]{:S(2)}, u32[]{:S(2)}) %all-to-all-start.2) | async-done | bytes 524320 | tf_op jit(solution)/shard_map/all_to_all | solution.py:346
  131.2 0.0 copy-done.3
  131.2 0.0 copy-start.5
  131.2 1.0 copy-done.5
  132.2 2.6 %finish.1 = (bf16[4,512,128]{2,1,0:T(8,128)(2,1)}, f32[4,512,128]{2,1,0:T(8,128)}) custom-call(f32[1]{0:T(128)S(6)} %copy.18.weight, s32[1]{0:T(128)} %bitcast.row_ref, bf16[512,512]{1,0:T(8,128)(2,1)S(1)} %copy-done.5, bf16[32,2,4,8,128]{4,3,2,1,0:T(8,128)(2,1)S(1)} %bitcast.22, bf16[32,2,4,8,128]{4,3,2,1,0:T(8,128)(2,1)S(1)} %bitcast.23, ...), custom_call_target="tpu_custom_call" | custom-call | flops 300000000 | bytes 6000000 | tf_op jit(solution)/shard_map/finish/pallas_call | solution.py:283
  (1 shorter events, 0.0 us)
Async XLA Ops:
  0.6 40.3 %copy-start.9 = (s32[2,8,4]{1,2,0:T(4,128)S(1)}, s32[2,8,4]{1,2,0:T(4,128)}, u32[]{:S(2)}) copy-start(s32[2,8,4]{1,2,0:T(4,128)} %param.13) | copy-start | bytes 772
  0.6 40.5 %copy-start.8 = (s32[5,8,4]{1,2,0:T(4,128)S(1)}, s32[5,8,4]{1,2,0:T(4,128)}, u32[]{:S(2)}) copy-start(s32[5,8,4]{1,2,0:T(4,128)} %param.15) | copy-start | bytes 1924
  0.7 41.6 %copy-start = (bf16[5,8,4,64,64]{4,3,2,1,0:T(8,128)(2,1)S(1)}, bf16[5,8,4,64,64]{4,3,2,1,0:T(8,128)(2,1)}, u32[]{:S(2)}) copy-start(bf16[5,8,4,64,64]{4,3,2,1,0:T(8,128)(2,1)} %b2.1) | copy-start | bytes 3932164
  0.7 27.5 %collective-permute-start.1 = (bf16[4,512,128]{2,1,0:T(8,128)(2,1)}, bf16[4,512,128]{2,1,0:T(8,128)(2,1)}, u32[]{:S(2)}, u32[]{:S(2)}) collective-permute-start(bf16[4,512,128]{2,1,0:T(8,128)(2,1)} %bitcast.18), channel_id=1, source_target_pairs={{1,0},{2,1},{3,2},{5,4},{6,5},{7,6},{9,8},{10,9},{11,10},{13,12},{... | collective-permute-start | bytes 1572872 | tf_op jit(solution)/shard_map/ppermute | solution.py:314
  2.9 25.3 %collective-permute-start = (bf16[4,512,128]{2,1,0:T(8,128)(2,1)}, bf16[4,512,128]{2,1,0:T(8,128)(2,1)}, u32[]{:S(2)}, u32[]{:S(2)}) collective-permute-start(bf16[4,512,128]{2,1,0:T(8,128)(2,1)} %bitcast.19), channel_id=1, source_target_pairs={{0,1},{1,2},{2,3},{4,5},{5,6},{6,7},{8,9},{9,10},{10,11},{12,13},{... | collective-permute-start | bytes 1572872 | tf_op jit(solution)/shard_map/ppermute | solution.py:313
  8.3 19.8 %all-to-all-start = ((bf16[32,64,128]{2,1,0:T(8,128)(2,1)}), bf16[32,64,128]{2,1,0:T(8,128)(2,1)S(1)}, u32[]{:S(2)}, u32[]{:S(2)}) async-start(bf16[32,64,128]{2,1,0:T(8,128)(2,1)} %bitcast.26), calls=%async_computation | async-start | bytes 1048576 | tf_op jit(solution)/shard_map/all_to_all | solution.py:318
  28.1 27.8 %copy-start.6 = (s32[3]{0:T(128)S(1)}, s32[3]{0:T(128)}, u32[]{:S(2)}) copy-start(s32[3]{0:T(128)} %offsets.1) | copy-start | bytes 40
  29.3 26.7 %copy-start.1 = (bf16[1,4,512,128]{3,2,1,0:T(8,128)(2,1)S(1)}, bf16[1,4,512,128]{3,2,1,0:T(8,128)(2,1)}, u32[]{:S(2)}) copy-start(bf16[1,4,512,128]{3,2,1,0:T(8,128)(2,1)} %param.9) | copy-start | bytes 1572868
  29.3 23.6 %collective-permute-start.2 = (bf16[8,128,128]{2,1,0:T(8,128)(2,1)}, bf16[8,128,128]{2,1,0:T(8,128)(2,1)}, u32[]{:S(2)}, u32[]{:S(2)}) collective-permute-start(bf16[8,128,128]{2,1,0:T(8,128)(2,1)} %get-tuple-element.22), channel_id=1, source_target_pairs={{0,32},{4,100},{8,40},{12,108},{16,48},{20,116},{24,56},{28,124},{... | collective-permute-start | bytes 786440 | tf_op jit(solution)/shard_map/ppermute | solution.py:324
  42.3 1.2 copy-start.2
  46.6 13.9 %copy-start.4 = (bf16[512,512]{1,0:T(8,128)(2,1)}, bf16[512,512]{1,0:T(8,128)(2,1)S(1)}, u32[]{:S(2)}) copy-start(bf16[512,512]{1,0:T(8,128)(2,1)S(1)} %get-tuple-element.17.sync2) | copy-start | bytes 1572868
  46.6 13.9 %collective-permute-start.3 = (bf16[8,128,128]{2,1,0:T(8,128)(2,1)S(1)}, bf16[8,128,128]{2,1,0:T(8,128)(2,1)S(1)}, u32[]{:S(2)}, u32[]{:S(2)}) collective-permute-start(bf16[8,128,128]{2,1,0:T(8,128)(2,1)S(1)} %get-tuple-element.23.mine), channel_id=1, source_target_pairs={{0,96},{4,36},{8,104},{12,44},{16,112},{20,52},{24,120},{28,60},{3... | collective-permute-start | bytes 786440 | tf_op jit(solution)/shard_map/ppermute | solution.py:335
  52.9 23.2 %collective-permute-start.4 = (bf16[8,128,128]{2,1,0:T(8,128)(2,1)}, bf16[8,128,128]{2,1,0:T(8,128)(2,1)S(1)}, u32[]{:S(2)}, u32[]{:S(2)}) collective-permute-start(bf16[8,128,128]{2,1,0:T(8,128)(2,1)} %collective-permute-done.2.pair), channel_id=1, source_target_pairs={{0,96},{4,36},{8,104},{12,44},{16,112},{20,52},{24,120},{28,60},{3... | collective-permute-start | bytes 786440 | tf_op jit(solution)/shard_map/ppermute | solution.py:325
  77.0 54.2 %copy-start.3 = (f32[1,4,512,128]{3,2,1,0:T(8,128)S(1)}, f32[1,4,512,128]{3,2,1,0:T(8,128)}, u32[]{:S(2)}) copy-start(f32[1,4,512,128]{3,2,1,0:T(8,128)} %param.10) | copy-start | bytes 3145732
  77.0 30.1 %collective-permute-start.5 = (bf16[32,2,32,128]{3,2,1,0:T(8,128)(2,1)S(1)}, bf16[32,2,32,128]{3,2,1,0:T(8,128)(2,1)S(1)}, u32[]{:S(2)}, u32[]{:S(2)}) collective-permute-start(bf16[32,2,32,128]{3,2,1,0:T(8,128)(2,1)S(1)} %far.3), channel_id=1, source_target_pairs={{0,32},{4,100},{8,40},{12,108},{16,48},{20,116},{24,56},{28,124},{... | collective-permute-start | bytes 1572872 | tf_op jit(solution)/shard_map/ppermute | solution.py:342
  107.1 0.8 copy-start.7
  107.9 23.3 %all-to-all-start.2 = ((bf16[32,64,128]{2,1,0:T(8,128)(2,1)}), bf16[32,64,128]{2,1,0:T(8,128)(2,1)S(1)}, u32[]{:S(2)}, u32[]{:S(2)}) async-start(bf16[32,64,128]{2,1,0:T(8,128)(2,1)} %bitcast.27), calls=%async_computation.2 | async-start | bytes 1048576 | tf_op jit(solution)/shard_map/all_to_all | solution.py:346
  131.2 1.0 copy-start.5

commit v3 on v2

--- a/solution.py
+++ b/solution.py
@@ -331,10 +331,10 @@
         route1_blocks,
         route2_blocks,
     )
-    ready, first = lax.optimization_barrier((mine, first))
-    cross = lax.ppermute(ready, "row", across)
     turned = jnp.swapaxes(route3_factors, 1, 2)
     base = local_terms(fleet_offsets, second, turned[0], field, before, after)
+    ready, base = lax.optimization_barrier((mine, base))
+    cross = lax.ppermute(ready, "row", across)
     acc = near(first, turned[1], mine, pair, cross)
     acc, base, opposite = lax.optimization_barrier((acc, base, opposite))
     theirs = far(1, first, turned[1], acc, opposite)

time: 136 us -> 137 us (level)
  the two profiles are of different devices: /device:TPU:33 before, /device:TPU:1 now
where the time goes in v3:
time: 137 us; the launch traced here: 136 us
  starting transfers between devices  50.1 us (37%)
  waiting for transfers between devices  31 us (23%)
  blocking collectives  27.6 us (20%)
  Pallas kernels  15.9 us (12%)
  local copies, waits for them, and re-layouts  9.53 us (7%)
  between operations  1.48 us (1%)
    all_to_all x1, blocking collectives, collect(): lax.all_to_all(value, 'row', 0, 0, tiled=True, axis_index_groups=groups)  27.6 us
    all_to_all x1, starting transfers between devices, collect(): lax.all_to_all(value, 'row', 0, 0, tiled=True, axis_index_groups=groups)  12.6 us
    ppermute x1, starting transfers between devices, local(): pair = lax.ppermute(other, 'row', swap)  11.5 us
    all_to_all x1, waiting for transfers between devices, collect(): lax.all_to_all(value, 'row', 0, 0, tiled=True, axis_index_groups=groups)  11 us
    all_to_all x1, waiting for transfers between devices, local(): lax.all_to_all(split, 'row', 0, 0, tiled=True, axis_index_groups=groups)  10.7 us
    all_to_all x1, starting transfers between devices, local(): lax.all_to_all(split, 'row', 0, 0, tiled=True, axis_index_groups=groups)  8.04 us
    unnamed x23, local copies, waits for them, and re-layouts  7.44 us
    ppermute x1, waiting for transfers between devices, local(): opposite = lax.ppermute(pair, 'row', across)  6.33 us
  transfers between devices with their start and end apart: 8, of which 4 were waited for; matrix products, arithmetic and copies ran while one was open for 3% of the time, Pallas kernels for 8%

profile of v3, /device:TPU:1, one launch (start us, length us, event | category | flops | bytes accessed | tf_op | source)
XLA Modules:
  0.0 135.6 jit_solution(12056121311349818384)
XLA Ops:
  0.6 0.0 copy-start
  0.6 5.4 %collective-permute-start = (bf16[4,512,128]{2,1,0:T(8,128)(2,1)}, bf16[4,512,128]{2,1,0:T(8,128)(2,1)}, u32[]{:S(2)}, u32[]{:S(2)}) collective-permute-start(bf16[4,512,128]{2,1,0:T(8,128)(2,1)} %bitcast.18), channel_id=1, source_target_pairs={{0,1},{1,2},{2,3},{4,5},{5,6},{6,7},{8,9},{9,10},{10,11},{12,13},{... | collective-permute-start | bytes 1572872 | tf_op jit(solution)/shard_map/ppermute | solution.py:313
  6.1 1.3 collective-permute-start.1
  7.4 1.9 %copy.17 = bf16[4,32,16,128]{3,2,0,1:T(8,128)(2,1)} copy(bf16[4,32,16,128]{3,2,1,0:T(8,128)(2,1)} %bitcast.20) | data formatting | bytes 1048576 | tf_op jit(solution)/shard_map/reshape;squeeze | solution.py:317
  9.3 8.0 %all-to-all-start = ((bf16[32,64,128]{2,1,0:T(8,128)(2,1)}), bf16[32,64,128]{2,1,0:T(8,128)(2,1)S(1)}, u32[]{:S(2)}, u32[]{:S(2)}) async-start(bf16[32,64,128]{2,1,0:T(8,128)(2,1)} %bitcast.26), calls=%async_computation | async-start | bytes 1048576 | tf_op jit(solution)/shard_map/all_to_all | solution.py:318
  17.3 1.0 copy.16
  18.3 10.7 %all-to-all-done.got = bf16[32,64,128]{2,1,0:T(8,128)(2,1)S(1)} async-done(((bf16[32,64,128]{2,1,0:T(8,128)(2,1)}), bf16[32,64,128]{2,1,0:T(8,128)(2,1)S(1)}, u32[]{:S(2)}, u32[]{:S(2)}) %all-to-all-start) | async-done | bytes 524320 | tf_op jit(solution)/shard_map/all_to_all | solution.py:318
  28.9 0.0 copy-start.2
  28.9 0.8 copy-done.2
  29.7 0.0 collective-permute-done.before
  29.7 0.0 collective-permute-done.1.after
  29.7 0.0 copy-start.3
  29.8 1.0 copy-done.3
  30.8 0.0 copy-start.1
  30.8 1.1 arrange.1
  31.9 11.5 %collective-permute-start.2 = (bf16[8,128,128]{2,1,0:T(8,128)(2,1)}, bf16[8,128,128]{2,1,0:T(8,128)(2,1)}, u32[]{:S(2)}, u32[]{:S(2)}) collective-permute-start(bf16[8,128,128]{2,1,0:T(8,128)(2,1)} %get-tuple-element.21), channel_id=1, source_target_pairs={{0,32},{4,100},{8,40},{12,108},{16,48},{20,116},{24,56},{28,124},{... | collective-permute-start | bytes 786440 | tf_op jit(solution)/shard_map/ppermute | solution.py:324
  43.5 0.8 copy.15
  44.3 0.1 reshape.30.cols2
  44.4 0.8 copy.14
  45.2 0.1 reshape.29.cols1
  45.3 0.0 copy-done
  45.3 0.0 copy-start.4
  45.3 1.2 copy-done.4
  46.5 0.0 copy-start.8
  46.5 3.1 %factors.1 = (bf16[512,2048]{1,0:T(8,128)(2,1)S(1)}, bf16[512,512]{1,0:T(8,128)(2,1)S(1)}, bf16[2,2,4,128,128]{4,3,2,1,0:T(8,128)(2,1)S(1)}) custom-call(s32[64]{0:T(128)S(1)} %reshape.29.cols1, s32[160]{0:T(256)S(1)} %reshape.30.cols2, s32[1]{0:T(128)} %bitcast.row_ref, bf16[2,8,4,64,64]{4,3,2,1,0:T(8,128)(2,1)S(1)} %copy-done.4, ...), custom_call_target="tpu_custom_call" | custom-call | flops 300000000 | bytes 8000000 | tf_op jit(solution)/shard_map/factors/pallas_call | solution.py:114
  49.6 0.0 copy-start.6
  49.6 0.0 copy-done.1
  49.6 0.0 copy-done.8
  49.6 4.7 %local_terms.1.base = f32[4,512,128]{2,1,0:T(8,128)S(1)} custom-call(s32[3]{0:T(128)S(1)} %copy-done.8, bf16[512,2048]{1,0:T(8,128)(2,1)S(1)} %get-tuple-element.22.second, bf16[128,128]{1,0:T(8,128)(2,1)S(1)} %get-tuple-element.32.r3, bf16[4,512,128]{2,1,0:T(8,128)(2,1)S(1)} %bitcast.21, bf16[4,512,128]{2,1,0:T(8,128)(2,1)} %collective-permute-done.before, ...), custom_call_target="tpu_custom_call" | custom-call | flops 1200000000 | bytes 5000000 | tf_op jit(solution)/shard_map/local_terms/pallas_call | solution.py:244
  54.3 0.0 copy-done.6
  54.3 5.2 %collective-permute-start.3 = (bf16[8,128,128]{2,1,0:T(8,128)(2,1)S(1)}, bf16[8,128,128]{2,1,0:T(8,128)(2,1)S(1)}, u32[]{:S(2)}, u32[]{:S(2)}) collective-permute-start(bf16[8,128,128]{2,1,0:T(8,128)(2,1)S(1)} %get-tuple-element.25.mine), channel_id=1, source_target_pairs={{0,96},{4,36},{8,104},{12,44},{16,112},{20,52},{24,120},{28,60},{3... | collective-permute-start | bytes 786440 | tf_op jit(solution)/shard_map/ppermute | solution.py:337
  59.5 0.0 collective-permute-done.2.pair
  59.5 4.0 %collective-permute-start.4 = (bf16[8,128,128]{2,1,0:T(8,128)(2,1)}, bf16[8,128,128]{2,1,0:T(8,128)(2,1)S(1)}, u32[]{:S(2)}, u32[]{:S(2)}) collective-permute-start(bf16[8,128,128]{2,1,0:T(8,128)(2,1)} %collective-permute-done.2.pair), channel_id=1, source_target_pairs={{0,96},{4,36},{8,104},{12,44},{16,112},{20,52},{24,120},{28,60},{3... | collective-permute-start | bytes 786440 | tf_op jit(solution)/shard_map/ppermute | solution.py:325
  63.5 3.1 %collective-permute-done.3.cross = bf16[8,128,128]{2,1,0:T(8,128)(2,1)S(1)} collective-permute-done((bf16[8,128,128]{2,1,0:T(8,128)(2,1)S(1)}, bf16[8,128,128]{2,1,0:T(8,128)(2,1)S(1)}, u32[]{:S(2)}, u32[]{:S(2)}) %collective-permute-start.3) | collective-permute-done | bytes 262176 | tf_op jit(solution)/shard_map/ppermute | solution.py:337
  66.6 2.7 %near.1.acc = f32[2,2,128,1024]{3,2,1,0:T(8,128)S(1)} custom-call(bf16[2,2,4,128,128]{4,3,2,1,0:T(8,128)(2,1)S(1)} %get-tuple-element.18.first, bf16[128,128]{1,0:T(8,128)(2,1)S(1)} %get-tuple-element.33.s3, bf16[8,128,128]{2,1,0:T(8,128)(2,1)S(1)} %get-tuple-element.25.mine, bf16[8,128,128]{2,1,0:T(8,128)(2,1)} %collective-permute-done.2.pair, ...), custom_call_target="tpu_custom_call" | custom-call | flops 700000000 | bytes 4000000 | tf_op jit(solution)/shard_map/near/pallas_call | solution.py:181
  69.3 6.3 %collective-permute-done.4.part = bf16[8,128,128]{2,1,0:T(8,128)(2,1)S(1)} collective-permute-done((bf16[8,128,128]{2,1,0:T(8,128)(2,1)}, bf16[8,128,128]{2,1,0:T(8,128)(2,1)S(1)}, u32[]{:S(2)}, u32[]{:S(2)}) %collective-permute-start.4) | collective-permute-done | bytes 262176 | tf_op jit(solution)/shard_map/ppermute | solution.py:325
  75.6 0.9 far.3
  76.5 0.0 copy-start.5
  76.5 2.1 %collective-permute-start.5 = (bf16[32,2,32,128]{3,2,1,0:T(8,128)(2,1)S(1)}, bf16[32,2,32,128]{3,2,1,0:T(8,128)(2,1)S(1)}, u32[]{:S(2)}, u32[]{:S(2)}) collective-permute-start(bf16[32,2,32,128]{3,2,1,0:T(8,128)(2,1)S(1)} %far.3), channel_id=1, source_target_pairs={{0,32},{4,100},{8,40},{12,108},{16,48},{20,116},{24,56},{28,124},{... | collective-permute-start | bytes 1572872 | tf_op jit(solution)/shard_map/ppermute | solution.py:342
  78.6 0.9 far.2
  79.4 27.6 %all_to_all.15 = bf16[32,64,128]{2,1,0:T(8,128)(2,1)S(1)} all-to-all(bf16[32,64,128]{2,1,0:T(8,128)(2,1)S(1)} %bitcast.24), channel_id=1, replica_groups={{0,4,8,12,16,20,24,28,128,132,136,140,144,148,152,156,256,260,264,268,2..., dimensions={0} | all-to-all | bytes 1048576 | tf_op jit(solution)/shard_map/all_to_all | solution.py:346
  107.0 0.0 collective-permute-done.5
  107.0 0.0 copy-start.9
  107.0 0.8 copy-done.9
  107.8 12.6 %all-to-all-start.2 = ((bf16[32,64,128]{2,1,0:T(8,128)(2,1)}), bf16[32,64,128]{2,1,0:T(8,128)(2,1)S(1)}, u32[]{:S(2)}, u32[]{:S(2)}) async-start(bf16[32,64,128]{2,1,0:T(8,128)(2,1)} %bitcast.27), calls=%async_computation.2 | async-start | bytes 1048576 | tf_op jit(solution)/shard_map/all_to_all | solution.py:346
  121.0 11.0 %all-to-all-done.2 = bf16[32,64,128]{2,1,0:T(8,128)(2,1)S(1)} async-done(((bf16[32,64,128]{2,1,0:T(8,128)(2,1)}), bf16[32,64,128]{2,1,0:T(8,128)(2,1)S(1)}, u32[]{:S(2)}, u32[]{:S(2)}) %all-to-all-start.2) | async-done | bytes 524320 | tf_op jit(solution)/shard_map/all_to_all | solution.py:346
  132.0 0.0 copy-done.5
  132.0 0.0 copy-start.7
  132.0 1.0 copy-done.7
  133.0 2.6 %finish.1 = (bf16[4,512,128]{2,1,0:T(8,128)(2,1)}, f32[4,512,128]{2,1,0:T(8,128)}) custom-call(f32[1]{0:T(128)S(6)} %copy.18.weight, s32[1]{0:T(128)} %bitcast.row_ref, bf16[512,512]{1,0:T(8,128)(2,1)S(1)} %copy-done.7, bf16[32,2,4,8,128]{4,3,2,1,0:T(8,128)(2,1)S(1)} %bitcast.22, bf16[32,2,4,8,128]{4,3,2,1,0:T(8,128)(2,1)S(1)} %bitcast.23, ...), custom_call_target="tpu_custom_call" | custom-call | flops 300000000 | bytes 6000000 | tf_op jit(solution)/shard_map/finish/pallas_call | solution.py:283
  (1 shorter events, 0.0 us)
Async XLA Ops:
  0.6 44.6 %copy-start = (bf16[5,8,4,64,64]{4,3,2,1,0:T(8,128)(2,1)S(1)}, bf16[5,8,4,64,64]{4,3,2,1,0:T(8,128)(2,1)}, u32[]{:S(2)}) copy-start(bf16[5,8,4,64,64]{4,3,2,1,0:T(8,128)(2,1)} %b2.1) | copy-start | bytes 3932164
  0.6 29.1 %collective-permute-start = (bf16[4,512,128]{2,1,0:T(8,128)(2,1)}, bf16[4,512,128]{2,1,0:T(8,128)(2,1)}, u32[]{:S(2)}, u32[]{:S(2)}) collective-permute-start(bf16[4,512,128]{2,1,0:T(8,128)(2,1)} %bitcast.18), channel_id=1, source_target_pairs={{0,1},{1,2},{2,3},{4,5},{5,6},{6,7},{8,9},{9,10},{10,11},{12,13},{... | collective-permute-start | bytes 1572872 | tf_op jit(solution)/shard_map/ppermute | solution.py:313
  6.1 23.7 %collective-permute-start.1 = (bf16[4,512,128]{2,1,0:T(8,128)(2,1)}, bf16[4,512,128]{2,1,0:T(8,128)(2,1)}, u32[]{:S(2)}, u32[]{:S(2)}) collective-permute-start(bf16[4,512,128]{2,1,0:T(8,128)(2,1)} %bitcast.19), channel_id=1, source_target_pairs={{1,0},{2,1},{3,2},{5,4},{6,5},{7,6},{9,8},{10,9},{11,10},{13,12},{... | collective-permute-start | bytes 1572872 | tf_op jit(solution)/shard_map/ppermute | solution.py:314
  9.3 19.7 %all-to-all-start = ((bf16[32,64,128]{2,1,0:T(8,128)(2,1)}), bf16[32,64,128]{2,1,0:T(8,128)(2,1)S(1)}, u32[]{:S(2)}, u32[]{:S(2)}) async-start(bf16[32,64,128]{2,1,0:T(8,128)(2,1)} %bitcast.26), calls=%async_computation | async-start | bytes 1048576 | tf_op jit(solution)/shard_map/all_to_all | solution.py:318
  28.9 0.8 copy-start.2
  29.7 1.0 copy-start.3
  30.8 18.8 %copy-start.1 = (bf16[1,4,512,128]{3,2,1,0:T(8,128)(2,1)S(1)}, bf16[1,4,512,128]{3,2,1,0:T(8,128)(2,1)}, u32[]{:S(2)}) copy-start(bf16[1,4,512,128]{3,2,1,0:T(8,128)(2,1)} %param.9) | copy-start | bytes 1572868
  31.9 27.6 %collective-permute-start.2 = (bf16[8,128,128]{2,1,0:T(8,128)(2,1)}, bf16[8,128,128]{2,1,0:T(8,128)(2,1)}, u32[]{:S(2)}, u32[]{:S(2)}) collective-permute-start(bf16[8,128,128]{2,1,0:T(8,128)(2,1)} %get-tuple-element.21), channel_id=1, source_target_pairs={{0,32},{4,100},{8,40},{12,108},{16,48},{20,116},{24,56},{28,124},{... | collective-permute-start | bytes 786440 | tf_op jit(solution)/shard_map/ppermute | solution.py:324
  45.3 1.2 copy-start.4
  46.5 3.1 %copy-start.8 = (s32[3]{0:T(128)S(1)}, s32[3]{0:T(128)}, u32[]{:S(2)}) copy-start(s32[3]{0:T(128)} %offsets.1) | copy-start | bytes 40
  49.6 4.7 %copy-start.6 = (bf16[512,512]{1,0:T(8,128)(2,1)}, bf16[512,512]{1,0:T(8,128)(2,1)S(1)}, u32[]{:S(2)}) copy-start(bf16[512,512]{1,0:T(8,128)(2,1)S(1)} %get-tuple-element.17.sync2) | copy-start | bytes 1572868
  54.3 12.3 %collective-permute-start.3 = (bf16[8,128,128]{2,1,0:T(8,128)(2,1)S(1)}, bf16[8,128,128]{2,1,0:T(8,128)(2,1)S(1)}, u32[]{:S(2)}, u32[]{:S(2)}) collective-permute-start(bf16[8,128,128]{2,1,0:T(8,128)(2,1)S(1)} %get-tuple-element.25.mine), channel_id=1, source_target_pairs={{0,96},{4,36},{8,104},{12,44},{16,112},{20,52},{24,120},{28,60},{3... | collective-permute-start | bytes 786440 | tf_op jit(solution)/shard_map/ppermute | solution.py:337
  59.5 16.1 %collective-permute-start.4 = (bf16[8,128,128]{2,1,0:T(8,128)(2,1)}, bf16[8,128,128]{2,1,0:T(8,128)(2,1)S(1)}, u32[]{:S(2)}, u32[]{:S(2)}) collective-permute-start(bf16[8,128,128]{2,1,0:T(8,128)(2,1)} %collective-permute-done.2.pair), channel_id=1, source_target_pairs={{0,96},{4,36},{8,104},{12,44},{16,112},{20,52},{24,120},{28,60},{3... | collective-permute-start | bytes 786440 | tf_op jit(solution)/shard_map/ppermute | solution.py:325
  76.5 55.5 %copy-start.5 = (f32[1,4,512,128]{3,2,1,0:T(8,128)S(1)}, f32[1,4,512,128]{3,2,1,0:T(8,128)}, u32[]{:S(2)}) copy-start(f32[1,4,512,128]{3,2,1,0:T(8,128)} %param.10) | copy-start | bytes 3145732
  76.5 30.5 %collective-permute-start.5 = (bf16[32,2,32,128]{3,2,1,0:T(8,128)(2,1)S(1)}, bf16[32,2,32,128]{3,2,1,0:T(8,128)(2,1)S(1)}, u32[]{:S(2)}, u32[]{:S(2)}) collective-permute-start(bf16[32,2,32,128]{3,2,1,0:T(8,128)(2,1)S(1)} %far.3), channel_id=1, source_target_pairs={{0,32},{4,100},{8,40},{12,108},{16,48},{20,116},{24,56},{28,124},{... | collective-permute-start | bytes 1572872 | tf_op jit(solution)/shard_map/ppermute | solution.py:342
  107.0 0.8 copy-start.9
  107.8 24.2 %all-to-all-start.2 = ((bf16[32,64,128]{2,1,0:T(8,128)(2,1)}), bf16[32,64,128]{2,1,0:T(8,128)(2,1)S(1)}, u32[]{:S(2)}, u32[]{:S(2)}) async-start(bf16[32,64,128]{2,1,0:T(8,128)(2,1)} %bitcast.27), calls=%async_computation.2 | async-start | bytes 1048576 | tf_op jit(solution)/shard_map/all_to_all | solution.py:346
  132.0 1.0 copy-start.7
